TPU v7x, 32 devices: a whole 2x2x4 slice. The times are simulated.
32 devices in a mesh: strike: 16 (over z, y, core), depth: 2 (over x).
Axes of the slice: x: 2, y: 2, z: 4, core: 2. Of those that a mesh axis runs over, the one named last changes fastest.
Arguments:
- velocity: float32 [3, 16, 32, 2048], P(None, 'depth', None, 'strike'), may hold values from -6 to 6
- stress: float32 [6, 16, 32, 2048], P(None, 'depth', None, 'strike'), may hold values from -6 to 6
- buoyancy: float32 [16, 32, 2048], P('depth', None, 'strike'), may hold values from 0.5 to 1
- lame_lambda: float32 [16, 32, 2048], P('depth', None, 'strike'), may hold values from 0.3 to 0.8
- shear_modulus: float32 [16, 32, 2048], P('depth', None, 'strike'), may hold values from 0.3 to 0.8
- past_rates: float32 [64, 16, 2048], P(None, 'depth', 'strike'), may hold values from -6 to 6
- memory_coefs: float32 [64], replicated, may hold values from 0.02 to 0.2
- prestress: float32 [16, 2048], P('depth', 'strike'), may hold values from -6 to 6
- fault_mask: int32 [16, 2048], P('depth', 'strike'), may hold values 0 or 1
Outputs:
- velocity_out: float32 [3, 16, 32, 2048], P(None, 'depth', None, 'strike')
- stress_out: float32 [6, 16, 32, 2048], P(None, 'depth', None, 'strike')
All inputs are finite; a program needn't handle non-finite values. No bound on the sum of `fault_mask` on one device may be relied on, other than what follows from the above.
Results may differ from a plain program's by a relative error of at most 0.0001.
Values sent between devices are 32-bit elements; how exact they have to be, the bound alone decides.
A program may use at most 64 MiB of HBM per device.

v0:
```python
import jax
import jax.numpy as jnp
from jax import lax
from jax.sharding import PartitionSpec as P

STEPS = 8


DT = 0.3
FRIC = 0.5


def passed_along(value, axis, steps):
    count = lax.axis_size(axis)
    pairs = [(source, (source + steps) % count) for source in range(count)]
    return lax.ppermute(value, axis, pairs)


def from_behind(array, axis, by):
    peers = lax.axis_size(axis)
    pairs = [(i, i + by) for i in range(peers) if 0 <= i + by < peers]
    return lax.ppermute(array, axis, pairs)


def ahead_y(f):
    return jnp.concatenate([f[:, 1:], jnp.zeros_like(f[:, :1])], axis=1)


def behind_y(f):
    return jnp.concatenate([jnp.zeros_like(f[:, :1]), f[:, :-1]], axis=1)


def front_strike(stack):
    return passed_along(stack, "strike", -1)


def back_strike(stack):
    return passed_along(stack, "strike", 1)


def front_depth(stack):
    return from_behind(stack, "depth", -1)


def back_depth(stack):
    return from_behind(stack, "depth", 1)


def per_device(
    velocity,
    stress,
    buoyancy,
    lame_lambda,
    shear_modulus,
    past_rates,
    memory_coefs,
    prestress,
    fault_mask,
):
    vx, vy, vz = (velocity[0], velocity[1], velocity[2])
    sxx, sxy, sxz, syz, szz, syy = (
        stress[0],
        stress[1],
        stress[2],
        stress[3],
        stress[4],
        stress[5],
    )
    center = vx.shape[1] // 2
    stiff = lame_lambda + 2.0 * shear_modulus
    history = past_rates
    for step in range(STEPS):
        got_fx = front_strike(jnp.stack([sxx[:, :, :1]]))
        got_bx = back_strike(jnp.stack([sxy[:, :, -1:], sxz[:, :, -1:]]))
        got_bz = back_depth(jnp.stack([sxz[-1:], syz[-1:]]))
        got_fz = front_depth(jnp.stack([szz[:1]]))
        sxx_next = jnp.concatenate([sxx[:, :, 1:], got_fx[0]], axis=2)
        sxy_prev = jnp.concatenate([got_bx[0], sxy[:, :, :-1]], axis=2)
        sxz_prev = jnp.concatenate([got_bx[1], sxz[:, :, :-1]], axis=2)
        sxz_below = jnp.concatenate([got_bz[0], sxz[:-1]], axis=0)
        syz_below = jnp.concatenate([got_bz[1], syz[:-1]], axis=0)
        szz_above = jnp.concatenate([szz[1:], got_fz[0]], axis=0)
        vx = vx + DT * buoyancy * (sxx_next - sxx + (sxy - behind_y(sxy)) + (sxz - sxz_below))
        vy = vy + DT * buoyancy * (sxy - sxy_prev + (ahead_y(syy) - syy) + (syz - syz_below))
        vz = vz + DT * buoyancy * (sxz - sxz_prev + (syz - behind_y(syz)) + (szz_above - szz))
        rate = vx[:, center + 1, :] - vx[:, center, :]
        memory = jnp.tensordot(memory_coefs, history, axes=1, precision=lax.Precision.HIGHEST)
        got_bx = back_strike(jnp.stack([vx[:, :, -1:]]))
        got_fx = front_strike(jnp.stack([vy[:, :, :1], vz[:, :, :1]]))
        got_bz = back_depth(jnp.stack([vz[-1:]]))
        got_fz = front_depth(jnp.stack([vx[:1], vy[:1]]))
        vx_prev = jnp.concatenate([got_bx[0], vx[:, :, :-1]], axis=2)
        vy_next = jnp.concatenate([vy[:, :, 1:], got_fx[0]], axis=2)
        vz_next = jnp.concatenate([vz[:, :, 1:], got_fx[1]], axis=2)
        vz_below = jnp.concatenate([got_bz[0], vz[:-1]], axis=0)
        vx_above = jnp.concatenate([vx[1:], got_fz[0]], axis=0)
        vy_above = jnp.concatenate([vy[1:], got_fz[1]], axis=0)
        strain_x = vx - vx_prev
        strain_y = vy - behind_y(vy)
        strain_z = vz - vz_below
        sxx = sxx + DT * (stiff * strain_x + lame_lambda * (strain_y + strain_z))
        syy = syy + DT * (stiff * strain_y + lame_lambda * (strain_x + strain_z))
        szz = szz + DT * (stiff * strain_z + lame_lambda * (strain_x + strain_y))
        sxy = sxy + DT * shear_modulus * (ahead_y(vx) - vx + (vy_next - vy))
        sxz = sxz + DT * shear_modulus * (vx_above - vx + (vz_next - vz))
        syz = syz + DT * shear_modulus * (vy_above - vy + (ahead_y(vz) - vz))
        fault = jnp.where(fault_mask == 1, prestress + FRIC * rate - memory, sxy[:, center, :])
        sxy = sxy.at[:, center, :].set(fault)
        if step + 1 < STEPS:
            history = passed_along(jnp.concatenate([rate[None], history[:-1]], axis=0), "strike", 1)
    return (jnp.stack([vx, vy, vz]), jnp.stack([sxx, sxy, sxz, syz, szz, syy]))


def solution(mesh):
    placed = (
        P(None, "depth", None, "strike"),
        P(None, "depth", None, "strike"),
        P("depth", None, "strike"),
        P("depth", None, "strike"),
        P("depth", None, "strike"),
        P(None, "depth", "strike"),
        P(),
        P("depth", "strike"),
        P("depth", "strike"),
    )
    return jax.shard_map(
        per_device,
        mesh=mesh,
        in_specs=placed,
        out_specs=(P(None, "depth", None, "strike"), P(None, "depth", None, "strike")),
        check_vma=False,
    )
```

profile of v0, /device:TPU:0, one launch (start us, length us, event | category | flops | bytes accessed | tf_op | source)
XLA Modules:
  0.0 217.9 jit_solution(864498194468929298)
XLA Ops:
  3.1 4.8 %collective-permute-start.1 = (f32[2,1,32,128]{3,2,1,0:T(8,128)S(1)}, f32[2,1,32,128]{3,2,1,0:T(8,128)S(1)}, u32[]{:S(2)}, u32[]{:S(2)}) collective-permute-start(f32[2,1,32,128]{3,2,1,0:T(8,128)S(1)} %stack.414), channel_id=1, source_target_pairs={{0,1},{2,3},{4,5},{6,7},{8,9},{10,11},{12,13},{14,15},{16,17},{18,... | collective-permute-start | bytes 98312 | tf_op jit(solution)/shard_map/ppermute | solution.py:22
  7.9 1.3 collective-permute-start.4
  9.5 3.8 %collective-permute-start = (f32[1,8,32,1]{2,1,3,0:T(8,128)S(1)}, f32[1,8,32,1]{2,1,3,0:T(8,128)S(1)}, u32[]{:S(2)}, u32[]{:S(2)}) collective-permute-start(f32[1,8,32,1]{2,1,3,0:T(8,128)S(1)} %bitcast.872), channel_id=1, source_target_pairs={{0,30},{2,0},{4,2},{6,4},{8,6},{10,8},{12,10},{14,12},{16,14},{18,... | collective-permute-start | bytes 3080 | tf_op jit(solution)/shard_map/ppermute | solution.py:16
  18.0 4.3 %collective-permute-start.7 = (f32[2,8,32,1]{2,1,3,0:T(8,128)S(1)}, f32[2,8,32,1]{2,1,3,0:T(8,128)S(1)}, u32[]{:S(2)}, u32[]{:S(2)}) collective-permute-start(f32[2,8,32,1]{2,1,3,0:T(8,128)S(1)} %pad_maximum_fusion.27), channel_id=1, source_target_pairs={{0,30},{2,0},{4,2},{6,4},{8,6},{10,8},{12,10},{14,12},{16,14},{18,... | collective-permute-start | bytes 6152 | tf_op jit(solution)/shard_map/ppermute | solution.py:16
  22.8 1.3 collective-permute-start.8
  24.1 4.5 %collective-permute-start.5 = (f32[1,1,32,128]{3,2,1,0:T(8,128)S(1)}, f32[1,1,32,128]{3,2,1,0:T(8,128)S(1)}, u32[]{:S(2)}, u32[]{:S(2)}) collective-permute-start(f32[1,1,32,128]{3,2,1,0:T(8,128)S(1)} %bitcast.831), channel_id=1, source_target_pairs={{0,1},{2,3},{4,5},{6,7},{8,9},{10,11},{12,13},{14,15},{16,17},{18,... | collective-permute-start | bytes 49160 | tf_op jit(solution)/shard_map/ppermute | solution.py:22
  32.2 4.3 %collective-permute-start.9 = (f32[2,1,32,128]{3,2,1,0:T(8,128)S(1)}, f32[2,1,32,128]{3,2,1,0:T(8,128)S(1)}, u32[]{:S(2)}, u32[]{:S(2)}) collective-permute-start(f32[2,1,32,128]{3,2,1,0:T(8,128)S(1)} %pad_maximum_fusion.12), channel_id=1, source_target_pairs={{0,1},{2,3},{4,5},{6,7},{8,9},{10,11},{12,13},{14,15},{16,17},{18,... | collective-permute-start | bytes 98312 | tf_op jit(solution)/shard_map/ppermute | solution.py:22
  36.9 1.3 collective-permute-start.12
  38.3 4.4 %collective-permute-start.6 = (f32[1,8,32,1]{2,1,3,0:T(8,128)S(1)}, f32[1,8,32,1]{2,1,3,0:T(8,128)S(1)}, u32[]{:S(2)}, u32[]{:S(2)}) collective-permute-start(f32[1,8,32,1]{2,1,3,0:T(8,128)S(1)} %bitcast.902), channel_id=1, source_target_pairs={{0,30},{2,0},{4,2},{6,4},{8,6},{10,8},{12,10},{14,12},{16,14},{18,... | collective-permute-start | bytes 3080 | tf_op jit(solution)/shard_map/ppermute | solution.py:16
  45.4 4.4 %collective-permute-start.15 = (f32[2,8,32,1]{2,1,3,0:T(8,128)S(1)}, f32[2,8,32,1]{2,1,3,0:T(8,128)S(1)}, u32[]{:S(2)}, u32[]{:S(2)}) collective-permute-start(f32[2,8,32,1]{2,1,3,0:T(8,128)S(1)} %pad_maximum_fusion.29), channel_id=1, source_target_pairs={{0,30},{2,0},{4,2},{6,4},{8,6},{10,8},{12,10},{14,12},{16,14},{18,... | collective-permute-start | bytes 6152 | tf_op jit(solution)/shard_map/ppermute | solution.py:16
  51.6 1.3 collective-permute-start.17
  52.9 4.5 %collective-permute-start.13 = (f32[1,1,32,128]{3,2,1,0:T(8,128)S(1)}, f32[1,1,32,128]{3,2,1,0:T(8,128)S(1)}, u32[]{:S(2)}, u32[]{:S(2)}) collective-permute-start(f32[1,1,32,128]{3,2,1,0:T(8,128)S(1)} %bitcast.832), channel_id=1, source_target_pairs={{0,1},{2,3},{4,5},{6,7},{8,9},{10,11},{12,13},{14,15},{16,17},{18,... | collective-permute-start | bytes 49160 | tf_op jit(solution)/shard_map/ppermute | solution.py:22
  59.5 1.3 multiply_add_fusion.16
  61.1 4.2 %collective-permute-start.18 = (f32[2,1,32,128]{3,2,1,0:T(8,128)S(1)}, f32[2,1,32,128]{3,2,1,0:T(8,128)S(1)}, u32[]{:S(2)}, u32[]{:S(2)}) collective-permute-start(f32[2,1,32,128]{3,2,1,0:T(8,128)S(1)} %pad_maximum_fusion.14), channel_id=1, source_target_pairs={{0,1},{2,3},{4,5},{6,7},{8,9},{10,11},{12,13},{14,15},{16,17},{18,... | collective-permute-start | bytes 98312 | tf_op jit(solution)/shard_map/ppermute | solution.py:22
  65.5 2.7 %collective-permute-start.14 = (f32[1,8,32,1]{2,1,3,0:T(8,128)S(1)}, f32[1,8,32,1]{2,1,3,0:T(8,128)S(1)}, u32[]{:S(2)}, u32[]{:S(2)}) collective-permute-start(f32[1,8,32,1]{2,1,3,0:T(8,128)S(1)} %bitcast.895), channel_id=1, source_target_pairs={{0,30},{2,0},{4,2},{6,4},{8,6},{10,8},{12,10},{14,12},{16,14},{18,... | collective-permute-start | bytes 3080 | tf_op jit(solution)/shard_map/ppermute | solution.py:16
  68.6 1.3 collective-permute-start.21
  72.6 4.2 %collective-permute-done.19 = f32[1,8,32,1]{2,1,3,0:T(8,128)S(1)} collective-permute-done((f32[1,8,32,1]{2,1,3,0:T(8,128)S(1)}, f32[1,8,32,1]{2,1,3,0:T(8,128)S(1)}, u32[]{:S(2)}, u32[]{:S(2)}) %collective-permute-start.19) | collective-permute-done | bytes 1056 | tf_op jit(solution)/shard_map/ppermute | solution.py:16
  79.5 1.3 collective-permute-start.26
  80.8 4.5 %collective-permute-start.22 = (f32[1,1,32,128]{3,2,1,0:T(8,128)S(1)}, f32[1,1,32,128]{3,2,1,0:T(8,128)S(1)}, u32[]{:S(2)}, u32[]{:S(2)}) collective-permute-start(f32[1,1,32,128]{3,2,1,0:T(8,128)S(1)} %bitcast.834), channel_id=1, source_target_pairs={{0,1},{2,3},{4,5},{6,7},{8,9},{10,11},{12,13},{14,15},{16,17},{18,... | collective-permute-start | bytes 49160 | tf_op jit(solution)/shard_map/ppermute | solution.py:22
  87.4 1.3 multiply_add_fusion.13
  89.1 4.2 %collective-permute-start.27 = (f32[2,1,32,128]{3,2,1,0:T(8,128)S(1)}, f32[2,1,32,128]{3,2,1,0:T(8,128)S(1)}, u32[]{:S(2)}, u32[]{:S(2)}) collective-permute-start(f32[2,1,32,128]{3,2,1,0:T(8,128)S(1)} %pad_maximum_fusion.16), channel_id=1, source_target_pairs={{0,1},{2,3},{4,5},{6,7},{8,9},{10,11},{12,13},{14,15},{16,17},{18,... | collective-permute-start | bytes 98312 | tf_op jit(solution)/shard_map/ppermute | solution.py:22
  94.0 1.3 collective-permute-start.30
  98.5 4.2 %collective-permute-done.28 = f32[1,8,32,1]{2,1,3,0:T(8,128)S(1)} collective-permute-done((f32[1,8,32,1]{2,1,3,0:T(8,128)S(1)}, f32[1,8,32,1]{2,1,3,0:T(8,128)S(1)}, u32[]{:S(2)}, u32[]{:S(2)}) %collective-permute-start.28) | collective-permute-done | bytes 1056 | tf_op jit(solution)/shard_map/ppermute | solution.py:16
  105.4 1.3 collective-permute-start.35
  106.7 4.5 %collective-permute-start.31 = (f32[1,1,32,128]{3,2,1,0:T(8,128)S(1)}, f32[1,1,32,128]{3,2,1,0:T(8,128)S(1)}, u32[]{:S(2)}, u32[]{:S(2)}) collective-permute-start(f32[1,1,32,128]{3,2,1,0:T(8,128)S(1)} %bitcast.835), channel_id=1, source_target_pairs={{0,1},{2,3},{4,5},{6,7},{8,9},{10,11},{12,13},{14,15},{16,17},{18,... | collective-permute-start | bytes 49160 | tf_op jit(solution)/shard_map/ppermute | solution.py:22
  113.2 1.3 multiply_add_fusion.10
  114.9 4.2 %collective-permute-start.36 = (f32[2,1,32,128]{3,2,1,0:T(8,128)S(1)}, f32[2,1,32,128]{3,2,1,0:T(8,128)S(1)}, u32[]{:S(2)}, u32[]{:S(2)}) collective-permute-start(f32[2,1,32,128]{3,2,1,0:T(8,128)S(1)} %pad_maximum_fusion.18), channel_id=1, source_target_pairs={{0,1},{2,3},{4,5},{6,7},{8,9},{10,11},{12,13},{14,15},{16,17},{18,... | collective-permute-start | bytes 98312 | tf_op jit(solution)/shard_map/ppermute | solution.py:22
  119.7 1.3 collective-permute-start.39
  124.2 4.2 %collective-permute-done.37 = f32[1,8,32,1]{2,1,3,0:T(8,128)S(1)} collective-permute-done((f32[1,8,32,1]{2,1,3,0:T(8,128)S(1)}, f32[1,8,32,1]{2,1,3,0:T(8,128)S(1)}, u32[]{:S(2)}, u32[]{:S(2)}) %collective-permute-start.37) | collective-permute-done | bytes 1056 | tf_op jit(solution)/shard_map/ppermute | solution.py:16
  131.1 1.3 collective-permute-start.44
  132.4 4.5 %collective-permute-start.40 = (f32[1,1,32,128]{3,2,1,0:T(8,128)S(1)}, f32[1,1,32,128]{3,2,1,0:T(8,128)S(1)}, u32[]{:S(2)}, u32[]{:S(2)}) collective-permute-start(f32[1,1,32,128]{3,2,1,0:T(8,128)S(1)} %bitcast.836), channel_id=1, source_target_pairs={{0,1},{2,3},{4,5},{6,7},{8,9},{10,11},{12,13},{14,15},{16,17},{18,... | collective-permute-start | bytes 49160 | tf_op jit(solution)/shard_map/ppermute | solution.py:22
  138.9 1.3 multiply_add_fusion.7
  140.6 4.2 %collective-permute-start.45 = (f32[2,1,32,128]{3,2,1,0:T(8,128)S(1)}, f32[2,1,32,128]{3,2,1,0:T(8,128)S(1)}, u32[]{:S(2)}, u32[]{:S(2)}) collective-permute-start(f32[2,1,32,128]{3,2,1,0:T(8,128)S(1)} %pad_maximum_fusion.20), channel_id=1, source_target_pairs={{0,1},{2,3},{4,5},{6,7},{8,9},{10,11},{12,13},{14,15},{16,17},{18,... | collective-permute-start | bytes 98312 | tf_op jit(solution)/shard_map/ppermute | solution.py:22
  145.4 1.3 collective-permute-start.48
  149.9 4.2 %collective-permute-done.46 = f32[1,8,32,1]{2,1,3,0:T(8,128)S(1)} collective-permute-done((f32[1,8,32,1]{2,1,3,0:T(8,128)S(1)}, f32[1,8,32,1]{2,1,3,0:T(8,128)S(1)}, u32[]{:S(2)}, u32[]{:S(2)}) %collective-permute-start.46) | collective-permute-done | bytes 1056 | tf_op jit(solution)/shard_map/ppermute | solution.py:16
  156.8 1.3 collective-permute-start.53
  158.1 4.5 %collective-permute-start.49 = (f32[1,1,32,128]{3,2,1,0:T(8,128)S(1)}, f32[1,1,32,128]{3,2,1,0:T(8,128)S(1)}, u32[]{:S(2)}, u32[]{:S(2)}) collective-permute-start(f32[1,1,32,128]{3,2,1,0:T(8,128)S(1)} %bitcast.837), channel_id=1, source_target_pairs={{0,1},{2,3},{4,5},{6,7},{8,9},{10,11},{12,13},{14,15},{16,17},{18,... | collective-permute-start | bytes 49160 | tf_op jit(solution)/shard_map/ppermute | solution.py:22
  164.6 1.3 multiply_add_fusion.4
  166.3 4.2 %collective-permute-start.54 = (f32[2,1,32,128]{3,2,1,0:T(8,128)S(1)}, f32[2,1,32,128]{3,2,1,0:T(8,128)S(1)}, u32[]{:S(2)}, u32[]{:S(2)}) collective-permute-start(f32[2,1,32,128]{3,2,1,0:T(8,128)S(1)} %pad_maximum_fusion.22), channel_id=1, source_target_pairs={{0,1},{2,3},{4,5},{6,7},{8,9},{10,11},{12,13},{14,15},{16,17},{18,... | collective-permute-start | bytes 98312 | tf_op jit(solution)/shard_map/ppermute | solution.py:22
  171.1 1.3 collective-permute-start.57
  175.6 4.2 %collective-permute-done.55 = f32[1,8,32,1]{2,1,3,0:T(8,128)S(1)} collective-permute-done((f32[1,8,32,1]{2,1,3,0:T(8,128)S(1)}, f32[1,8,32,1]{2,1,3,0:T(8,128)S(1)}, u32[]{:S(2)}, u32[]{:S(2)}) %collective-permute-start.55) | collective-permute-done | bytes 1056 | tf_op jit(solution)/shard_map/ppermute | solution.py:16
  182.4 1.3 collective-permute-start.62
  183.7 4.8 %collective-permute-start.58 = (f32[1,1,32,128]{3,2,1,0:T(8,128)S(1)}, f32[1,1,32,128]{3,2,1,0:T(8,128)S(1)}, u32[]{:S(2)}, u32[]{:S(2)}) collective-permute-start(f32[1,1,32,128]{3,2,1,0:T(8,128)S(1)} %bitcast.838), channel_id=1, source_target_pairs={{0,1},{2,3},{4,5},{6,7},{8,9},{10,11},{12,13},{14,15},{16,17},{18,... | collective-permute-start | bytes 49160 | tf_op jit(solution)/shard_map/ppermute | solution.py:22
  190.3 1.3 multiply_add_fusion.2
  192.0 4.2 %collective-permute-start.63 = (f32[2,1,32,128]{3,2,1,0:T(8,128)S(1)}, f32[2,1,32,128]{3,2,1,0:T(8,128)S(1)}, u32[]{:S(2)}, u32[]{:S(2)}) collective-permute-start(f32[2,1,32,128]{3,2,1,0:T(8,128)S(1)} %pad_maximum_fusion.24), channel_id=1, source_target_pairs={{0,1},{2,3},{4,5},{6,7},{8,9},{10,11},{12,13},{14,15},{16,17},{18,... | collective-permute-start | bytes 98312 | tf_op jit(solution)/shard_map/ppermute | solution.py:22
  200.1 4.4 %collective-permute-done.64 = f32[2,8,32,1]{2,1,3,0:T(8,128)S(1)} collective-permute-done((f32[2,8,32,1]{2,1,3,0:T(8,128)S(1)}, f32[2,8,32,1]{2,1,3,0:T(8,128)S(1)}, u32[]{:S(2)}, u32[]{:S(2)}) %collective-permute-start.64) | collective-permute-done | bytes 2080 | tf_op jit(solution)/shard_map/ppermute | solution.py:16
  205.9 1.3 collective-permute-start.70
  208.9 4.5 %collective-permute-start.67 = (f32[1,1,32,128]{3,2,1,0:T(8,128)S(1)}, f32[1,1,32,128]{3,2,1,0:T(8,128)S(1)}, u32[]{:S(2)}, u32[]{:S(2)}) collective-permute-start(f32[1,1,32,128]{3,2,1,0:T(8,128)S(1)} %bitcast.833), channel_id=1, source_target_pairs={{0,1},{2,3},{4,5},{6,7},{8,9},{10,11},{12,13},{14,15},{16,17},{18,... | collective-permute-start | bytes 49160 | tf_op jit(solution)/shard_map/ppermute | solution.py:22
  (561 shorter events, 70.8 us)
Async XLA Ops:
  2.6 12.3 %collective-permute-start.3 = (f32[2,8,32,1]{2,1,3,0:T(8,128)S(1)}, f32[2,8,32,1]{2,1,3,0:T(8,128)S(1)}, u32[]{:S(2)}, u32[]{:S(2)}) collective-permute-start(f32[2,8,32,1]{2,1,3,0:T(8,128)S(1)} %pad_maximum_fusion.26), channel_id=1, source_target_pairs={{0,2},{2,4},{4,6},{6,8},{8,10},{10,12},{12,14},{14,16},{16,18},{18... | collective-permute-start | bytes 6152 | tf_op jit(solution)/shard_map/ppermute | solution.py:16
  3.1 12.0 %collective-permute-start.1 = (f32[2,1,32,128]{3,2,1,0:T(8,128)S(1)}, f32[2,1,32,128]{3,2,1,0:T(8,128)S(1)}, u32[]{:S(2)}, u32[]{:S(2)}) collective-permute-start(f32[2,1,32,128]{3,2,1,0:T(8,128)S(1)} %stack.414), channel_id=1, source_target_pairs={{0,1},{2,3},{4,5},{6,7},{8,9},{10,11},{12,13},{14,15},{16,17},{18,... | collective-permute-start | bytes 98312 | tf_op jit(solution)/shard_map/ppermute | solution.py:22
  7.9 7.2 %collective-permute-start.4 = (f32[1,1,32,128]{3,2,1,0:T(8,128)S(1)}, f32[1,1,32,128]{3,2,1,0:T(8,128)S(1)}, u32[]{:S(2)}, u32[]{:S(2)}) collective-permute-start(f32[1,1,32,128]{3,2,1,0:T(8,128)S(1)} %slice.1237), channel_id=1, source_target_pairs={{1,0},{3,2},{5,4},{7,6},{9,8},{11,10},{13,12},{15,14},{17,16},{19,... | collective-permute-start | bytes 49160 | tf_op jit(solution)/shard_map/ppermute | solution.py:22
  18.0 10.8 %collective-permute-start.7 = (f32[2,8,32,1]{2,1,3,0:T(8,128)S(1)}, f32[2,8,32,1]{2,1,3,0:T(8,128)S(1)}, u32[]{:S(2)}, u32[]{:S(2)}) collective-permute-start(f32[2,8,32,1]{2,1,3,0:T(8,128)S(1)} %pad_maximum_fusion.27), channel_id=1, source_target_pairs={{0,30},{2,0},{4,2},{6,4},{8,6},{10,8},{12,10},{14,12},{16,14},{18,... | collective-permute-start | bytes 6152 | tf_op jit(solution)/shard_map/ppermute | solution.py:16
  22.4 6.2 %collective-permute-start.2 = (f32[1,8,32,1]{2,1,3,0:T(8,128)S(1)}, f32[1,8,32,1]{2,1,3,0:T(8,128)S(1)}, u32[]{:S(2)}, u32[]{:S(2)}) collective-permute-start(f32[1,8,32,1]{2,1,3,0:T(8,128)S(1)} %bitcast.873), channel_id=1, source_target_pairs={{0,2},{2,4},{4,6},{6,8},{8,10},{10,12},{12,14},{14,16},{16,18},{18... | collective-permute-start | bytes 3080 | tf_op jit(solution)/shard_map/ppermute | solution.py:16
  22.8 6.3 %collective-permute-start.8 = (f32[2,1,32,128]{3,2,1,0:T(8,128)S(1)}, f32[2,1,32,128]{3,2,1,0:T(8,128)S(1)}, u32[]{:S(2)}, u32[]{:S(2)}) collective-permute-start(f32[2,1,32,128]{3,2,1,0:T(8,128)S(1)} %pad_maximum_fusion.11), channel_id=1, source_target_pairs={{1,0},{3,2},{5,4},{7,6},{9,8},{11,10},{13,12},{15,14},{17,16},{19,... | collective-permute-start | bytes 98312 | tf_op jit(solution)/shard_map/ppermute | solution.py:22
  32.2 12.3 %collective-permute-start.9 = (f32[2,1,32,128]{3,2,1,0:T(8,128)S(1)}, f32[2,1,32,128]{3,2,1,0:T(8,128)S(1)}, u32[]{:S(2)}, u32[]{:S(2)}) collective-permute-start(f32[2,1,32,128]{3,2,1,0:T(8,128)S(1)} %pad_maximum_fusion.12), channel_id=1, source_target_pairs={{0,1},{2,3},{4,5},{6,7},{8,9},{10,11},{12,13},{14,15},{16,17},{18,... | collective-permute-start | bytes 98312 | tf_op jit(solution)/shard_map/ppermute | solution.py:22
  36.8 7.4 %collective-permute-start.11 = (f32[2,8,32,1]{2,1,3,0:T(8,128)S(1)}, f32[2,8,32,1]{2,1,3,0:T(8,128)S(1)}, u32[]{:S(2)}, u32[]{:S(2)}) collective-permute-start(f32[2,8,32,1]{2,1,3,0:T(8,128)S(1)} %pad_maximum_fusion.28), channel_id=1, source_target_pairs={{0,2},{2,4},{4,6},{6,8},{8,10},{10,12},{12,14},{14,16},{16,18},{18... | collective-permute-start | bytes 6152 | tf_op jit(solution)/shard_map/ppermute | solution.py:16
  36.9 8.0 %collective-permute-start.12 = (f32[1,1,32,128]{3,2,1,0:T(8,128)S(1)}, f32[1,1,32,128]{3,2,1,0:T(8,128)S(1)}, u32[]{:S(2)}, u32[]{:S(2)}) collective-permute-start(f32[1,1,32,128]{3,2,1,0:T(8,128)S(1)} %bitcast.830), channel_id=1, source_target_pairs={{1,0},{3,2},{5,4},{7,6},{9,8},{11,10},{13,12},{15,14},{17,16},{19,... | collective-permute-start | bytes 49160 | tf_op jit(solution)/shard_map/ppermute | solution.py:22
  43.6 26.5 %collective-permute-start.16 = (f32[64,8,128]{2,1,0:T(8,128)}, f32[64,8,128]{2,1,0:T(8,128)S(1)}, u32[]{:S(2)}, u32[]{:S(2)}) collective-permute-start(f32[64,8,128]{2,1,0:T(8,128)} %pad_maximum_fusion.1), channel_id=1, source_target_pairs={{0,2},{2,4},{4,6},{6,8},{8,10},{10,12},{12,14},{14,16},{16,18},{18... | collective-permute-start | bytes 786440 | tf_op jit(solution)/shard_map/ppermute | solution.py:16
  45.4 12.2 %collective-permute-start.15 = (f32[2,8,32,1]{2,1,3,0:T(8,128)S(1)}, f32[2,8,32,1]{2,1,3,0:T(8,128)S(1)}, u32[]{:S(2)}, u32[]{:S(2)}) collective-permute-start(f32[2,8,32,1]{2,1,3,0:T(8,128)S(1)} %pad_maximum_fusion.29), channel_id=1, source_target_pairs={{0,30},{2,0},{4,2},{6,4},{8,6},{10,8},{12,10},{14,12},{16,14},{18,... | collective-permute-start | bytes 6152 | tf_op jit(solution)/shard_map/ppermute | solution.py:16
  49.9 7.5 %collective-permute-start.10 = (f32[1,8,32,1]{2,1,3,0:T(8,128)S(1)}, f32[1,8,32,1]{2,1,3,0:T(8,128)S(1)}, u32[]{:S(2)}, u32[]{:S(2)}) collective-permute-start(f32[1,8,32,1]{2,1,3,0:T(8,128)S(1)} %bitcast.875), channel_id=1, source_target_pairs={{0,2},{2,4},{4,6},{6,8},{8,10},{10,12},{12,14},{14,16},{16,18},{18... | collective-permute-start | bytes 3080 | tf_op jit(solution)/shard_map/ppermute | solution.py:16
  51.6 6.3 %collective-permute-start.17 = (f32[2,1,32,128]{3,2,1,0:T(8,128)S(1)}, f32[2,1,32,128]{3,2,1,0:T(8,128)S(1)}, u32[]{:S(2)}, u32[]{:S(2)}) collective-permute-start(f32[2,1,32,128]{3,2,1,0:T(8,128)S(1)} %pad_maximum_fusion.13), channel_id=1, source_target_pairs={{1,0},{3,2},{5,4},{7,6},{9,8},{11,10},{13,12},{15,14},{17,16},{19,... | collective-permute-start | bytes 98312 | tf_op jit(solution)/shard_map/ppermute | solution.py:22
  61.1 8.9 %collective-permute-start.18 = (f32[2,1,32,128]{3,2,1,0:T(8,128)S(1)}, f32[2,1,32,128]{3,2,1,0:T(8,128)S(1)}, u32[]{:S(2)}, u32[]{:S(2)}) collective-permute-start(f32[2,1,32,128]{3,2,1,0:T(8,128)S(1)} %pad_maximum_fusion.14), channel_id=1, source_target_pairs={{0,1},{2,3},{4,5},{6,7},{8,9},{10,11},{12,13},{14,15},{16,17},{18,... | collective-permute-start | bytes 98312 | tf_op jit(solution)/shard_map/ppermute | solution.py:22
  68.6 8.7 %collective-permute-start.21 = (f32[1,1,32,128]{3,2,1,0:T(8,128)S(1)}, f32[1,1,32,128]{3,2,1,0:T(8,128)S(1)}, u32[]{:S(2)}, u32[]{:S(2)}) collective-permute-start(f32[1,1,32,128]{3,2,1,0:T(8,128)S(1)} %bitcast.824), channel_id=1, source_target_pairs={{1,0},{3,2},{5,4},{7,6},{9,8},{11,10},{13,12},{15,14},{17,16},{19,... | collective-permute-start | bytes 49160 | tf_op jit(solution)/shard_map/ppermute | solution.py:22
  70.6 6.4 %collective-permute-start.20 = (f32[2,8,32,1]{2,1,3,0:T(8,128)S(1)}, f32[2,8,32,1]{2,1,3,0:T(8,128)S(1)}, u32[]{:S(2)}, u32[]{:S(2)}) collective-permute-start(f32[2,8,32,1]{2,1,3,0:T(8,128)S(1)} %pad_maximum_fusion.30), channel_id=1, source_target_pairs={{0,2},{2,4},{4,6},{6,8},{8,10},{10,12},{12,14},{14,16},{16,18},{18... | collective-permute-start | bytes 6152 | tf_op jit(solution)/shard_map/ppermute | solution.py:16
  72.6 22.9 %collective-permute-start.25 = (f32[64,8,128]{2,1,0:T(8,128)}, f32[64,8,128]{2,1,0:T(8,128)S(1)}, u32[]{:S(2)}, u32[]{:S(2)}) collective-permute-start(f32[64,8,128]{2,1,0:T(8,128)} %pad_maximum_fusion.2), channel_id=1, source_target_pairs={{0,2},{2,4},{4,6},{6,8},{8,10},{10,12},{12,14},{14,16},{16,18},{18... | collective-permute-start | bytes 786440 | tf_op jit(solution)/shard_map/ppermute | solution.py:16
  77.9 7.5 %collective-permute-start.24 = (f32[2,8,32,1]{2,1,3,0:T(8,128)S(1)}, f32[2,8,32,1]{2,1,3,0:T(8,128)S(1)}, u32[]{:S(2)}, u32[]{:S(2)}) collective-permute-start(f32[2,8,32,1]{2,1,3,0:T(8,128)S(1)} %pad_maximum_fusion.31), channel_id=1, source_target_pairs={{0,30},{2,0},{4,2},{6,4},{8,6},{10,8},{12,10},{14,12},{16,14},{18,... | collective-permute-start | bytes 6152 | tf_op jit(solution)/shard_map/ppermute | solution.py:16
  79.5 6.2 %collective-permute-start.26 = (f32[2,1,32,128]{3,2,1,0:T(8,128)S(1)}, f32[2,1,32,128]{3,2,1,0:T(8,128)S(1)}, u32[]{:S(2)}, u32[]{:S(2)}) collective-permute-start(f32[2,1,32,128]{3,2,1,0:T(8,128)S(1)} %pad_maximum_fusion.15), channel_id=1, source_target_pairs={{1,0},{3,2},{5,4},{7,6},{9,8},{11,10},{13,12},{15,14},{17,16},{19,... | collective-permute-start | bytes 98312 | tf_op jit(solution)/shard_map/ppermute | solution.py:22
  89.1 6.4 %collective-permute-start.27 = (f32[2,1,32,128]{3,2,1,0:T(8,128)S(1)}, f32[2,1,32,128]{3,2,1,0:T(8,128)S(1)}, u32[]{:S(2)}, u32[]{:S(2)}) collective-permute-start(f32[2,1,32,128]{3,2,1,0:T(8,128)S(1)} %pad_maximum_fusion.16), channel_id=1, source_target_pairs={{0,1},{2,3},{4,5},{6,7},{8,9},{10,11},{12,13},{14,15},{16,17},{18,... | collective-permute-start | bytes 98312 | tf_op jit(solution)/shard_map/ppermute | solution.py:22
  94.0 9.2 %collective-permute-start.30 = (f32[1,1,32,128]{3,2,1,0:T(8,128)S(1)}, f32[1,1,32,128]{3,2,1,0:T(8,128)S(1)}, u32[]{:S(2)}, u32[]{:S(2)}) collective-permute-start(f32[1,1,32,128]{3,2,1,0:T(8,128)S(1)} %bitcast.825), channel_id=1, source_target_pairs={{1,0},{3,2},{5,4},{7,6},{9,8},{11,10},{13,12},{15,14},{17,16},{19,... | collective-permute-start | bytes 49160 | tf_op jit(solution)/shard_map/ppermute | solution.py:22
  96.0 6.8 %collective-permute-start.29 = (f32[2,8,32,1]{2,1,3,0:T(8,128)S(1)}, f32[2,8,32,1]{2,1,3,0:T(8,128)S(1)}, u32[]{:S(2)}, u32[]{:S(2)}) collective-permute-start(f32[2,8,32,1]{2,1,3,0:T(8,128)S(1)} %pad_maximum_fusion.32), channel_id=1, source_target_pairs={{0,2},{2,4},{4,6},{6,8},{8,10},{10,12},{12,14},{14,16},{16,18},{18... | collective-permute-start | bytes 6152 | tf_op jit(solution)/shard_map/ppermute | solution.py:16
  98.5 22.7 %collective-permute-start.34 = (f32[64,8,128]{2,1,0:T(8,128)}, f32[64,8,128]{2,1,0:T(8,128)S(1)}, u32[]{:S(2)}, u32[]{:S(2)}) collective-permute-start(f32[64,8,128]{2,1,0:T(8,128)} %pad_maximum_fusion.3), channel_id=1, source_target_pairs={{0,2},{2,4},{4,6},{6,8},{8,10},{10,12},{12,14},{14,16},{16,18},{18... | collective-permute-start | bytes 786440 | tf_op jit(solution)/shard_map/ppermute | solution.py:16
  103.7 7.5 %collective-permute-start.33 = (f32[2,8,32,1]{2,1,3,0:T(8,128)S(1)}, f32[2,8,32,1]{2,1,3,0:T(8,128)S(1)}, u32[]{:S(2)}, u32[]{:S(2)}) collective-permute-start(f32[2,8,32,1]{2,1,3,0:T(8,128)S(1)} %pad_maximum_fusion.33), channel_id=1, source_target_pairs={{0,30},{2,0},{4,2},{6,4},{8,6},{10,8},{12,10},{14,12},{16,14},{18,... | collective-permute-start | bytes 6152 | tf_op jit(solution)/shard_map/ppermute | solution.py:16
  114.9 6.2 %collective-permute-start.36 = (f32[2,1,32,128]{3,2,1,0:T(8,128)S(1)}, f32[2,1,32,128]{3,2,1,0:T(8,128)S(1)}, u32[]{:S(2)}, u32[]{:S(2)}) collective-permute-start(f32[2,1,32,128]{3,2,1,0:T(8,128)S(1)} %pad_maximum_fusion.18), channel_id=1, source_target_pairs={{0,1},{2,3},{4,5},{6,7},{8,9},{10,11},{12,13},{14,15},{16,17},{18,... | collective-permute-start | bytes 98312 | tf_op jit(solution)/shard_map/ppermute | solution.py:22
  119.7 9.2 %collective-permute-start.39 = (f32[1,1,32,128]{3,2,1,0:T(8,128)S(1)}, f32[1,1,32,128]{3,2,1,0:T(8,128)S(1)}, u32[]{:S(2)}, u32[]{:S(2)}) collective-permute-start(f32[1,1,32,128]{3,2,1,0:T(8,128)S(1)} %bitcast.826), channel_id=1, source_target_pairs={{1,0},{3,2},{5,4},{7,6},{9,8},{11,10},{13,12},{15,14},{17,16},{19,... | collective-permute-start | bytes 49160 | tf_op jit(solution)/shard_map/ppermute | solution.py:22
  121.7 6.9 %collective-permute-start.38 = (f32[2,8,32,1]{2,1,3,0:T(8,128)S(1)}, f32[2,8,32,1]{2,1,3,0:T(8,128)S(1)}, u32[]{:S(2)}, u32[]{:S(2)}) collective-permute-start(f32[2,8,32,1]{2,1,3,0:T(8,128)S(1)} %pad_maximum_fusion.34), channel_id=1, source_target_pairs={{0,2},{2,4},{4,6},{6,8},{8,10},{10,12},{12,14},{14,16},{16,18},{18... | collective-permute-start | bytes 6152 | tf_op jit(solution)/shard_map/ppermute | solution.py:16
  124.1 22.7 %collective-permute-start.43 = (f32[64,8,128]{2,1,0:T(8,128)}, f32[64,8,128]{2,1,0:T(8,128)S(1)}, u32[]{:S(2)}, u32[]{:S(2)}) collective-permute-start(f32[64,8,128]{2,1,0:T(8,128)} %pad_maximum_fusion.4), channel_id=1, source_target_pairs={{0,2},{2,4},{4,6},{6,8},{8,10},{10,12},{12,14},{14,16},{16,18},{18... | collective-permute-start | bytes 786440 | tf_op jit(solution)/shard_map/ppermute | solution.py:16
  129.4 7.5 %collective-permute-start.42 = (f32[2,8,32,1]{2,1,3,0:T(8,128)S(1)}, f32[2,8,32,1]{2,1,3,0:T(8,128)S(1)}, u32[]{:S(2)}, u32[]{:S(2)}) collective-permute-start(f32[2,8,32,1]{2,1,3,0:T(8,128)S(1)} %pad_maximum_fusion.35), channel_id=1, source_target_pairs={{0,30},{2,0},{4,2},{6,4},{8,6},{10,8},{12,10},{14,12},{16,14},{18,... | collective-permute-start | bytes 6152 | tf_op jit(solution)/shard_map/ppermute | solution.py:16
  131.1 6.2 %collective-permute-start.44 = (f32[2,1,32,128]{3,2,1,0:T(8,128)S(1)}, f32[2,1,32,128]{3,2,1,0:T(8,128)S(1)}, u32[]{:S(2)}, u32[]{:S(2)}) collective-permute-start(f32[2,1,32,128]{3,2,1,0:T(8,128)S(1)} %pad_maximum_fusion.19), channel_id=1, source_target_pairs={{1,0},{3,2},{5,4},{7,6},{9,8},{11,10},{13,12},{15,14},{17,16},{19,... | collective-permute-start | bytes 98312 | tf_op jit(solution)/shard_map/ppermute | solution.py:22
  140.6 6.2 %collective-permute-start.45 = (f32[2,1,32,128]{3,2,1,0:T(8,128)S(1)}, f32[2,1,32,128]{3,2,1,0:T(8,128)S(1)}, u32[]{:S(2)}, u32[]{:S(2)}) collective-permute-start(f32[2,1,32,128]{3,2,1,0:T(8,128)S(1)} %pad_maximum_fusion.20), channel_id=1, source_target_pairs={{0,1},{2,3},{4,5},{6,7},{8,9},{10,11},{12,13},{14,15},{16,17},{18,... | collective-permute-start | bytes 98312 | tf_op jit(solution)/shard_map/ppermute | solution.py:22
  145.4 9.2 %collective-permute-start.48 = (f32[1,1,32,128]{3,2,1,0:T(8,128)S(1)}, f32[1,1,32,128]{3,2,1,0:T(8,128)S(1)}, u32[]{:S(2)}, u32[]{:S(2)}) collective-permute-start(f32[1,1,32,128]{3,2,1,0:T(8,128)S(1)} %bitcast.827), channel_id=1, source_target_pairs={{1,0},{3,2},{5,4},{7,6},{9,8},{11,10},{13,12},{15,14},{17,16},{19,... | collective-permute-start | bytes 49160 | tf_op jit(solution)/shard_map/ppermute | solution.py:22
  147.4 6.8 %collective-permute-start.47 = (f32[2,8,32,1]{2,1,3,0:T(8,128)S(1)}, f32[2,8,32,1]{2,1,3,0:T(8,128)S(1)}, u32[]{:S(2)}, u32[]{:S(2)}) collective-permute-start(f32[2,8,32,1]{2,1,3,0:T(8,128)S(1)} %pad_maximum_fusion.36), channel_id=1, source_target_pairs={{0,2},{2,4},{4,6},{6,8},{8,10},{10,12},{12,14},{14,16},{16,18},{18... | collective-permute-start | bytes 6152 | tf_op jit(solution)/shard_map/ppermute | solution.py:16
  149.8 22.7 %collective-permute-start.52 = (f32[64,8,128]{2,1,0:T(8,128)}, f32[64,8,128]{2,1,0:T(8,128)S(1)}, u32[]{:S(2)}, u32[]{:S(2)}) collective-permute-start(f32[64,8,128]{2,1,0:T(8,128)} %pad_maximum_fusion.5), channel_id=1, source_target_pairs={{0,2},{2,4},{4,6},{6,8},{8,10},{10,12},{12,14},{14,16},{16,18},{18... | collective-permute-start | bytes 786440 | tf_op jit(solution)/shard_map/ppermute | solution.py:16
  155.1 7.5 %collective-permute-start.51 = (f32[2,8,32,1]{2,1,3,0:T(8,128)S(1)}, f32[2,8,32,1]{2,1,3,0:T(8,128)S(1)}, u32[]{:S(2)}, u32[]{:S(2)}) collective-permute-start(f32[2,8,32,1]{2,1,3,0:T(8,128)S(1)} %pad_maximum_fusion.37), channel_id=1, source_target_pairs={{0,30},{2,0},{4,2},{6,4},{8,6},{10,8},{12,10},{14,12},{16,14},{18,... | collective-permute-start | bytes 6152 | tf_op jit(solution)/shard_map/ppermute | solution.py:16
  156.8 6.2 %collective-permute-start.53 = (f32[2,1,32,128]{3,2,1,0:T(8,128)S(1)}, f32[2,1,32,128]{3,2,1,0:T(8,128)S(1)}, u32[]{:S(2)}, u32[]{:S(2)}) collective-permute-start(f32[2,1,32,128]{3,2,1,0:T(8,128)S(1)} %pad_maximum_fusion.21), channel_id=1, source_target_pairs={{1,0},{3,2},{5,4},{7,6},{9,8},{11,10},{13,12},{15,14},{17,16},{19,... | collective-permute-start | bytes 98312 | tf_op jit(solution)/shard_map/ppermute | solution.py:22
  166.3 6.2 %collective-permute-start.54 = (f32[2,1,32,128]{3,2,1,0:T(8,128)S(1)}, f32[2,1,32,128]{3,2,1,0:T(8,128)S(1)}, u32[]{:S(2)}, u32[]{:S(2)}) collective-permute-start(f32[2,1,32,128]{3,2,1,0:T(8,128)S(1)} %pad_maximum_fusion.22), channel_id=1, source_target_pairs={{0,1},{2,3},{4,5},{6,7},{8,9},{10,11},{12,13},{14,15},{16,17},{18,... | collective-permute-start | bytes 98312 | tf_op jit(solution)/shard_map/ppermute | solution.py:22
  171.1 9.2 %collective-permute-start.57 = (f32[1,1,32,128]{3,2,1,0:T(8,128)S(1)}, f32[1,1,32,128]{3,2,1,0:T(8,128)S(1)}, u32[]{:S(2)}, u32[]{:S(2)}) collective-permute-start(f32[1,1,32,128]{3,2,1,0:T(8,128)S(1)} %bitcast.828), channel_id=1, source_target_pairs={{1,0},{3,2},{5,4},{7,6},{9,8},{11,10},{13,12},{15,14},{17,16},{19,... | collective-permute-start | bytes 49160 | tf_op jit(solution)/shard_map/ppermute | solution.py:22
  173.1 6.9 %collective-permute-start.56 = (f32[2,8,32,1]{2,1,3,0:T(8,128)S(1)}, f32[2,8,32,1]{2,1,3,0:T(8,128)S(1)}, u32[]{:S(2)}, u32[]{:S(2)}) collective-permute-start(f32[2,8,32,1]{2,1,3,0:T(8,128)S(1)} %pad_maximum_fusion.38), channel_id=1, source_target_pairs={{0,2},{2,4},{4,6},{6,8},{8,10},{10,12},{12,14},{14,16},{16,18},{18... | collective-permute-start | bytes 6152 | tf_op jit(solution)/shard_map/ppermute | solution.py:16
  175.5 22.7 %collective-permute-start.61 = (f32[64,8,128]{2,1,0:T(8,128)}, f32[64,8,128]{2,1,0:T(8,128)S(1)}, u32[]{:S(2)}, u32[]{:S(2)}) collective-permute-start(f32[64,8,128]{2,1,0:T(8,128)} %pad_maximum_fusion.6), channel_id=1, source_target_pairs={{0,2},{2,4},{4,6},{6,8},{8,10},{10,12},{12,14},{14,16},{16,18},{18... | collective-permute-start | bytes 786440 | tf_op jit(solution)/shard_map/ppermute | solution.py:16
  180.8 7.7 %collective-permute-start.60 = (f32[2,8,32,1]{2,1,3,0:T(8,128)S(1)}, f32[2,8,32,1]{2,1,3,0:T(8,128)S(1)}, u32[]{:S(2)}, u32[]{:S(2)}) collective-permute-start(f32[2,8,32,1]{2,1,3,0:T(8,128)S(1)} %pad_maximum_fusion.39), channel_id=1, source_target_pairs={{0,30},{2,0},{4,2},{6,4},{8,6},{10,8},{12,10},{14,12},{16,14},{18,... | collective-permute-start | bytes 6152 | tf_op jit(solution)/shard_map/ppermute | solution.py:16
  182.4 6.4 %collective-permute-start.62 = (f32[2,1,32,128]{3,2,1,0:T(8,128)S(1)}, f32[2,1,32,128]{3,2,1,0:T(8,128)S(1)}, u32[]{:S(2)}, u32[]{:S(2)}) collective-permute-start(f32[2,1,32,128]{3,2,1,0:T(8,128)S(1)} %pad_maximum_fusion.23), channel_id=1, source_target_pairs={{1,0},{3,2},{5,4},{7,6},{9,8},{11,10},{13,12},{15,14},{17,16},{19,... | collective-permute-start | bytes 98312 | tf_op jit(solution)/shard_map/ppermute | solution.py:22
  192.0 6.2 %collective-permute-start.63 = (f32[2,1,32,128]{3,2,1,0:T(8,128)S(1)}, f32[2,1,32,128]{3,2,1,0:T(8,128)S(1)}, u32[]{:S(2)}, u32[]{:S(2)}) collective-permute-start(f32[2,1,32,128]{3,2,1,0:T(8,128)S(1)} %pad_maximum_fusion.24), channel_id=1, source_target_pairs={{0,1},{2,3},{4,5},{6,7},{8,9},{10,11},{12,13},{14,15},{16,17},{18,... | collective-permute-start | bytes 98312 | tf_op jit(solution)/shard_map/ppermute | solution.py:22
  196.8 8.7 %collective-permute-start.65 = (f32[1,1,32,128]{3,2,1,0:T(8,128)S(1)}, f32[1,1,32,128]{3,2,1,0:T(8,128)S(1)}, u32[]{:S(2)}, u32[]{:S(2)}) collective-permute-start(f32[1,1,32,128]{3,2,1,0:T(8,128)S(1)} %bitcast.829), channel_id=1, source_target_pairs={{1,0},{3,2},{5,4},{7,6},{9,8},{11,10},{13,12},{15,14},{17,16},{19,... | collective-permute-start | bytes 49160 | tf_op jit(solution)/shard_map/ppermute | solution.py:22
  200.1 15.5 %collective-permute-start.69 = (f32[64,8,128]{2,1,0:T(8,128)}, f32[64,8,128]{2,1,0:T(8,128)}, u32[]{:S(2)}, u32[]{:S(2)}) collective-permute-start(f32[64,8,128]{2,1,0:T(8,128)} %pad_maximum_fusion.7), channel_id=1, source_target_pairs={{0,2},{2,4},{4,6},{6,8},{8,10},{10,12},{12,14},{14,16},{16,18},{18... | collective-permute-start | bytes 786440 | tf_op jit(solution)/shard_map/ppermute | solution.py:16
  205.8 7.8 %collective-permute-start.68 = (f32[2,8,32,1]{2,1,3,0:T(8,128)S(1)}, f32[2,8,32,1]{2,1,3,0:T(8,128)S(1)}, u32[]{:S(2)}, u32[]{:S(2)}) collective-permute-start(f32[2,8,32,1]{2,1,3,0:T(8,128)S(1)} %pad_maximum_fusion.41), channel_id=1, source_target_pairs={{0,30},{2,0},{4,2},{6,4},{8,6},{10,8},{12,10},{14,12},{16,14},{18,... | collective-permute-start | bytes 6152 | tf_op jit(solution)/shard_map/ppermute | solution.py:16
  205.9 8.1 %collective-permute-start.70 = (f32[2,1,32,128]{3,2,1,0:T(8,128)S(1)}, f32[2,1,32,128]{3,2,1,0:T(8,128)S(1)}, u32[]{:S(2)}, u32[]{:S(2)}) collective-permute-start(f32[2,1,32,128]{3,2,1,0:T(8,128)S(1)} %pad_maximum_fusion.25), channel_id=1, source_target_pairs={{1,0},{3,2},{5,4},{7,6},{9,8},{11,10},{13,12},{15,14},{17,16},{19,... | collective-permute-start | bytes 98312 | tf_op jit(solution)/shard_map/ppermute | solution.py:22
  207.3 6.2 %collective-permute-start.66 = (f32[1,8,32,1]{2,1,3,0:T(8,128)S(1)}, f32[1,8,32,1]{2,1,3,0:T(8,128)S(1)}, u32[]{:S(2)}, u32[]{:S(2)}) collective-permute-start(f32[1,8,32,1]{2,1,3,0:T(8,128)S(1)} %bitcast.877), channel_id=1, source_target_pairs={{0,2},{2,4},{4,6},{6,8},{8,10},{10,12},{12,14},{14,16},{16,18},{18... | collective-permute-start | bytes 3080 | tf_op jit(solution)/shard_map/ppermute | solution.py:16
  (55 other events, 172.7 us)
where the time goes:
time: 219 us; the launch traced here: 218 us
  starting transfers between devices  118 us (54%)
  local copies, waits for them, and re-layouts  37.7 us (17%)
  waiting for transfers between devices  34.1 us (16%)
  other arithmetic  21.9 us (10%)
  between operations  3.59 us (2%)
  matrix products  3.07 us (1%)
    ppermute x32, starting transfers between devices, from_behind(): return lax.ppermute(array, axis, pairs)  91.6 us
    ppermute x39, waiting for transfers between devices, passed_along(): return lax.ppermute(value, axis, pairs)  26 us
    ppermute x39, starting transfers between devices, passed_along(): return lax.ppermute(value, axis, pairs)  26 us
    ppermute x32, waiting for transfers between devices, from_behind(): return lax.ppermute(array, axis, pairs)  8.04 us
    slice x24, local copies, waits for them, and re-layouts, ahead_y(): return jnp.concatenate([f[:, 1:], jnp.zeros_like(f[:, :1])], axis=1)  7.99 us
    add x7, other arithmetic, per_device(): syy = syy + DT * (stiff * strain_y + lame_lambda * (strain_x + strain_z))  7.56 us
    unnamed x60, local copies, waits for them, and re-layouts  7.22 us
    concatenate x7, other arithmetic, per_device(): jnp.concatenate([rate[None], history[:-1]], axis=0)  5.05 us
  transfers between devices with their start and end apart: 71, of which 15 were waited for; matrix products, arithmetic and copies ran while one was open for 22% of the time, Pallas kernels for 0%

commit v1 on v0

v1 whole, which is shorter than its diff:
```python
import functools

import jax
import jax.numpy as jnp
from jax import lax
from jax.experimental import pallas as pl
from jax.experimental.pallas import tpu as pltpu
from jax.sharding import PartitionSpec as P

STEPS = 8
DT = 0.3
FRIC = 0.5
GROUP = 16

MESH = pl.DeviceIdType.MESH
F32 = jnp.float32


def kernel(
    n_strike,
    n_depth,
    vel_in,
    str_in,
    buoy,
    lam_ref,
    mu_ref,
    past,
    coefs,
    prestress,
    mask,
    vel,
    stress,
    pack0,
    pack1,
    accs,
    stage,
    got_r,
    got_l,
    got_rb,
    got_lt,
    got_t,
    got_b,
    got_acc,
    col_state,
    col_coef,
    layer_state,
    layer_coef,
    send_sem,
    recv_sem,
):
    nz, ny, nx = buoy.shape
    y0 = ny // 2
    hist = past.shape[0]
    s = lax.axis_index("strike")
    d = lax.axis_index("depth")
    left = lax.rem(s + n_strike - 1, n_strike)
    right = lax.rem(s + 1, n_strike)
    has_b = d > 0
    has_t = d < n_depth - 1
    below = jnp.maximum(d - 1, 0)
    above = jnp.minimum(d + 1, n_depth - 1)

    lane = lax.broadcasted_iota(jnp.int32, (ny, nx), 1)
    row = lax.broadcasted_iota(jnp.int32, (ny, nx), 0)
    first_lane, last_lane = lane == 0, lane == nx - 1
    first_row, last_row = row == 0, row == ny - 1

    def lanes_down(f, by):
        return pltpu.roll(f, (nx - by) % nx, 1)

    def ahead_x(f, column):
        return jnp.where(last_lane, column, pltpu.roll(f, nx - 1, 1))

    def behind_x(f, column):
        return jnp.where(first_lane, column, pltpu.roll(f, 1, 1))

    def ahead_y(f):
        return jnp.where(last_row, 0.0, pltpu.roll(f, ny - 1, 0))

    def behind_y(f):
        return jnp.where(first_row, 0.0, pltpu.roll(f, 1, 0))

    def col(f, group, z):
        at = group * GROUP + z
        return f[:, at : at + 1]

    def pack(columns):
        out = jnp.zeros((ny, nx), F32)
        for at, column in columns:
            out = jnp.where(lane == at, column, out)
        return out

    def copy(kind, slot, source=None):
        src, dst, to = (
            (pack0.at[slot], got_r.at[slot], (left, d)),
            (pack1.at[slot], got_l.at[slot], (right, d)),
            (pack0.at[slot], got_rb.at[slot], (left, above)),
            (pack1.at[slot], got_lt.at[slot], (right, below)),
            (vel.at[:, 0], got_t.at[slot], (s, below)),
            (vel.at[:, nz - 1], got_b.at[slot], (s, above)),
            (accs.at[slot], got_acc.at[slot], (right, d)),
        )[kind]
        return pltpu.make_async_remote_copy(
            src_ref=src if source is None else source,
            dst_ref=dst,
            send_sem=send_sem.at[kind, slot],
            recv_sem=recv_sem.at[kind, slot],
            device_id={"strike": to[0], "depth": to[1]},
            device_id_type=MESH,
        )

    sent_when = (None, None, has_t, has_b, has_b, has_t, None)
    got_when = (None, None, has_b, has_t, has_t, has_b, None)

    def guarded(condition, action):
        if condition is None:
            action()
        else:
            pl.when(condition)(action)

    def start(kind, slot, source=None):
        guarded(sent_when[kind], lambda: copy(kind, slot, source).start())

    def finish(kind, slot, source=None):
        guarded(got_when[kind], lambda: copy(kind, slot, source).wait_recv())
        guarded(sent_when[kind], lambda: copy(kind, slot, source).wait_send())

    barrier = pltpu.get_barrier_semaphore()

    def greet(strike, depth):
        pl.semaphore_signal(
            barrier,
            inc=1,
            device_id={"strike": strike, "depth": depth},
            device_id_type=MESH,
        )

    greet(left, d)
    greet(right, d)

    @pl.when(has_t)
    def _():
        greet(s, above)
        greet(left, above)

    @pl.when(has_b)
    def _():
        greet(s, below)
        greet(right, below)

    @pl.when(jnp.logical_not(has_t))
    def _():
        got_t[...] = jnp.zeros_like(got_t)
        got_lt[...] = jnp.zeros_like(got_lt)

    @pl.when(jnp.logical_not(has_b))
    def _():
        got_b[...] = jnp.zeros_like(got_b)
        got_rb[...] = jnp.zeros_like(got_rb)

    stage[0, 0] = str_in[4, 0]
    stage[0, 1] = lam_ref[0]
    stage[0, 2] = mu_ref[0]
    stage[1, 0] = str_in[2, nz - 1]
    stage[1, 1] = str_in[3, nz - 1]
    stage[1, 2] = mu_ref[nz - 1]
    heads, tails = [], []
    for z in range(nz):
        heads += [
            (z, str_in[0, z][:, :1]),
            (GROUP + z, lam_ref[z][:, :1]),
            (2 * GROUP + z, mu_ref[z][:, :1]),
        ]
        slides = mask[z : z + 1, :].astype(F32)
        tails += [
            (z, str_in[1, z][:, nx - 1 :]),
            (GROUP + z, str_in[2, z][:, nx - 1 :]),
            (2 * GROUP + z, mu_ref[z][:, nx - 1 :]),
            (3 * GROUP + z, slides[:, nx - 1 :]),
        ]
    pack0[1] = pack(heads)
    pack1[1] = pack(tails)
    pl.semaphore_wait(
        barrier, 2 + 2 * has_t.astype(jnp.int32) + 2 * has_b.astype(jnp.int32)
    )
    opening = ((4, stage.at[0]), (5, stage.at[1]), (0, None), (1, None))
    for kind, source in opening:
        start(kind, 1, source)

    vel[...] = vel_in[...]
    stress[...] = str_in[...]

    def add_past(m, sums):
        plane = past[m]
        return tuple(sums[t] + coefs[m + t] * plane for t in range(STEPS))

    sums = lax.fori_loop(
        0,
        hist - STEPS + 1,
        add_past,
        tuple(jnp.zeros((nz, nx), F32) for _ in range(STEPS)),
    )
    sums = list(sums)
    for m in range(hist - STEPS + 1, hist):
        for t in range(hist - m):
            sums[t] = sums[t] + coefs[m + t] * past[m]
    for t in range(STEPS):
        got_acc[1, t] = sums[t]

    for kind, source in opening:
        finish(kind, 1, source)
    r_init, l_init = got_r[1], got_l[1]
    col_state[0] = r_init
    col_state[1] = l_init
    col_state[2] = lanes_down(l_init, GROUP)
    col_coef[0] = lanes_down(r_init, GROUP)
    col_coef[1] = lanes_down(r_init, 2 * GROUP)
    col_coef[2] = lanes_down(l_init, 2 * GROUP)
    col_coef[3] = lanes_down(l_init, 3 * GROUP)
    layer_state[0] = got_t[1, 0]
    layer_state[1] = got_b[1, 0]
    layer_state[2] = got_b[1, 1]
    layer_coef[0] = got_t[1, 1]
    layer_coef[1] = got_t[1, 2]
    layer_coef[2] = got_b[1, 2]

    def step(j, carry):
        slot = lax.rem(j, 2)
        other = 1 - slot
        sxx_r, sxy_l, sxz_l = col_state[0], col_state[1], col_state[2]

        def velocity(z):
            sxx, sxy, sxz = stress[0, z], stress[1, z], stress[2, z]
            syz, szz, syy = stress[3, z], stress[4, z], stress[5, z]
            sxz_below = layer_state[1] if z == 0 else stress[2, z - 1]
            syz_below = layer_state[2] if z == 0 else stress[3, z - 1]
            szz_above = layer_state[0] if z == nz - 1 else stress[4, z + 1]
            scale = DT * buoy[z]
            vel[0, z] = vel[0, z] + scale * (
                ahead_x(sxx, col(sxx_r, 0, z)) - sxx + (sxy - behind_y(sxy)) + (sxz - sxz_below)
            )
            vel[1, z] = vel[1, z] + scale * (
                sxy - behind_x(sxy, col(sxy_l, 0, z)) + (ahead_y(syy) - syy) + (syz - syz_below)
            )
            vel[2, z] = vel[2, z] + scale * (
                sxz - behind_x(sxz, col(sxz_l, 0, z)) + (syz - behind_y(syz)) + (szz_above - szz)
            )

        velocity(0)
        start(4, slot)
        velocity(nz - 1)
        start(5, slot)
        for z in range(1, nz - 1):
            velocity(z)

        rate = jnp.concatenate(
            [vel[0, z, y0 + 1 : y0 + 2] - vel[0, z, y0 : y0 + 1] for z in range(nz)], axis=0
        )
        fault = prestress[...] + FRIC * rate - got_acc[other, 0]

        for t in range(STEPS - 1):
            accs[slot, t] = got_acc[other, t + 1] + coefs[t] * rate
        accs[slot, STEPS - 1] = jnp.zeros((nz, nx), F32)

        heads, tails = [], []
        for z in range(nz):
            for c in range(3):
                f = vel[c, z]
                heads.append((c * GROUP + z, f[:, :1]))
                tails.append((c * GROUP + z, f[:, nx - 1 :]))
            tails.append((3 * GROUP + z, fault[z : z + 1, nx - 1 :]))
        own_first = pack(heads)
        own_last = pack(tails)
        pack0[slot] = own_first
        pack1[slot] = own_last
        start(1, slot)
        start(0, slot)
        start(2, slot)
        start(3, slot)

        @pl.when(j < STEPS - 1)
        def _():
            copy(6, slot).start()

        for kind in range(6):
            finish(kind, slot)

        @pl.when(j < STEPS - 1)
        def _():
            finish(6, slot)

        got_first = jnp.where(
            lane == 2 * GROUP - 1, lanes_down(got_rb[slot], nz), got_r[slot]
        )
        got_last = jnp.where(lane == nz, pltpu.roll(got_lt[slot], nz, 1), got_l[slot])

        lam_r, mu_r, mu_l = col_coef[0], col_coef[1], col_coef[2]
        strain_x = got_first - own_last
        strain_y = lanes_down(got_first - behind_y(got_first), GROUP)
        strain_z = lanes_down(got_first - pltpu.roll(got_first, 1, 1), 2 * GROUP)
        col_state[0] = sxx_r + DT * (
            (lam_r + 2.0 * mu_r) * strain_x + lam_r * (strain_y + strain_z)
        )
        jump = own_first - got_last
        sheared = sxy_l + DT * mu_l * (ahead_y(got_last) - got_last + lanes_down(jump, GROUP))
        col_state[1] = jnp.where(
            jnp.logical_and(row == y0, col_coef[3] > 0.5),
            lanes_down(got_last, 3 * GROUP),
            sheared,
        )
        col_state[2] = sxz_l + DT * mu_l * (
            lanes_down(got_last, 1) - got_last + lanes_down(jump, 2 * GROUP)
        )

        top_x, top_y, top_z = got_t[slot, 0], got_t[slot, 1], got_t[slot, 2]
        lam_t, mu_t = layer_coef[0], layer_coef[1]
        layer_state[0] = layer_state[0] + DT * (
            (lam_t + 2.0 * mu_t) * (top_z - vel[2, nz - 1])
            + lam_t * (top_x - behind_x(top_x, col(got_last, 0, nz)) + (top_y - behind_y(top_y)))
        )
        low_x, low_y, low_z = got_b[slot, 0], got_b[slot, 1], got_b[slot, 2]
        low_mu = DT * layer_coef[2]
        layer_state[1] = layer_state[1] + low_mu * (
            vel[0, 0] - low_x + (ahead_x(low_z, col(got_first, 2, -1)) - low_z)
        )
        layer_state[2] = layer_state[2] + low_mu * (
            vel[1, 0] - low_y + (ahead_y(low_z) - low_z)
        )

        for z in range(nz):
            vx, vy, vz = vel[0, z], vel[1, z], vel[2, z]
            vz_below = low_z if z == 0 else vel[2, z - 1]
            vx_above = top_x if z == nz - 1 else vel[0, z + 1]
            vy_above = top_y if z == nz - 1 else vel[1, z + 1]
            lam, mu = DT * lam_ref[z], DT * mu_ref[z]
            twice = 2.0 * mu
            strain_x = vx - behind_x(vx, col(got_last, 0, z))
            strain_y = vy - behind_y(vy)
            strain_z = vz - vz_below
            spread = lam * (strain_x + strain_y + strain_z)
            stress[0, z] = stress[0, z] + (twice * strain_x + spread)
            stress[5, z] = stress[5, z] + (twice * strain_y + spread)
            stress[4, z] = stress[4, z] + (twice * strain_z + spread)
            sxy = stress[1, z] + mu * (
                ahead_y(vx) - vx + (ahead_x(vy, col(got_first, 1, z)) - vy)
            )
            stress[1, z] = sxy
            stress[1, z, y0 : y0 + 1] = jnp.where(
                mask[z : z + 1] == 1, fault[z : z + 1], sxy[y0 : y0 + 1]
            )
            stress[2, z] = stress[2, z] + mu * (
                vx_above - vx + (ahead_x(vz, col(got_first, 2, z)) - vz)
            )
            stress[3, z] = stress[3, z] + mu * (vy_above - vy + (ahead_y(vz) - vz))
        return carry

    lax.fori_loop(0, STEPS, step, 0)


def per_device(n_strike, n_depth, *args):
    nz, ny, nx = args[2].shape
    slab = (2, ny, nx)
    vmem = pl.BlockSpec(memory_space=pltpu.VMEM)
    specs = [vmem] * len(args)
    specs[6] = pl.BlockSpec(memory_space=pltpu.SMEM)
    return pl.pallas_call(
        functools.partial(kernel, n_strike, n_depth),
        out_shape=tuple(jax.ShapeDtypeStruct(a.shape, a.dtype) for a in args[:2]),
        in_specs=specs,
        out_specs=(vmem, vmem),
        scratch_shapes=[
            pltpu.VMEM(slab, F32),
            pltpu.VMEM(slab, F32),
            pltpu.VMEM((2, STEPS, nz, nx), F32),
            pltpu.VMEM((2, 3, ny, nx), F32),
            pltpu.VMEM(slab, F32),
            pltpu.VMEM(slab, F32),
            pltpu.VMEM(slab, F32),
            pltpu.VMEM(slab, F32),
            pltpu.VMEM((2, 3, ny, nx), F32),
            pltpu.VMEM((2, 3, ny, nx), F32),
            pltpu.VMEM((2, STEPS, nz, nx), F32),
            pltpu.VMEM((3, ny, nx), F32),
            pltpu.VMEM((4, ny, nx), F32),
            pltpu.VMEM((3, ny, nx), F32),
            pltpu.VMEM((3, ny, nx), F32),
            pltpu.SemaphoreType.DMA((7, 2)),
            pltpu.SemaphoreType.DMA((7, 2)),
        ],
        compiler_params=pltpu.CompilerParams(collective_id=0, has_side_effects=True),
    )(*args)


def solution(mesh):
    wide = P(None, "depth", None, "strike")
    placed = (
        wide,
        wide,
        P("depth", None, "strike"),
        P("depth", None, "strike"),
        P("depth", None, "strike"),
        P(None, "depth", "strike"),
        P(),
        P("depth", "strike"),
        P("depth", "strike"),
    )
    return jax.shard_map(
        functools.partial(per_device, mesh.shape["strike"], mesh.shape["depth"]),
        mesh=mesh,
        in_specs=placed,
        out_specs=(wide, wide),
        check_vma=False,
    )
```

time: 219 us -> 58.8 us (0.27)
  starting transfers between devices: 118 us -> 0 us
  Pallas kernels: 0 us -> 55.2 us
  local copies, waits for them, and re-layouts: 37.7 us -> 2.72 us
  waiting for transfers between devices: 34.1 us -> 0 us
  other arithmetic: 21.9 us -> 0 us
  matrix products: 3.07 us -> 0 us
  between operations: 3.59 us -> 0.65 us
    ppermute x71 -> x0, starting transfers between devices: 118 us -> none  [the longest x32 91.6 us: from_behind(): return lax.ppermute(array, axis, pairs)]
    pallas_call x0 -> x1, Pallas kernels: none -> 55.2 us  [per_device(): pl.pallas_call(functools.partial(kernel, n_strike, n_depth), out_shape=tu...]
    ppermute x71 -> x0, waiting for transfers between devices: 34.1 us -> none  [the longest x39 26 us: passed_along(): return lax.ppermute(value, axis, pairs)]
    slice x244 -> x0, local copies, waits for them, and re-layouts: 23.3 us -> none  [the longest x24 7.99 us: ahead_y(): return jnp.concatenate([f[:, 1:], jnp.zeros_like(f[:, :1])], axis=1)]
    add x30 -> x0, other arithmetic: 15.2 us -> none  [the longest x7 7.56 us: per_device(): syy = syy + DT * (stiff * strain_y + lame_lambda * (strain_x + strain_z))]
    squeeze x66 -> x0, local copies, waits for them, and re-layouts: 7.01 us -> none  [the longest x16 1.16 us: per_device(): sxy_prev = jnp.concatenate([got_bx[0], sxy[:, :, :-1]], axis=2)]
    concatenate x10 -> x0, other arithmetic: 5.08 us -> none  [the longest x7 5.05 us: per_device(): jnp.concatenate([rate[None], history[:-1]], axis=0)]
    unnamed x60 -> x4, local copies, waits for them, and re-layouts: 7.22 us -> 2.72 us
  transfers between devices with their start and end apart: 71 -> 0, of which waited for: 15 -> 0; matrix products, arithmetic and copies ran while one was open for 22% -> 0% of each run, Pallas kernels for 0% -> 0%
where the time goes in v1:
time: 58.8 us; the launch traced here: 58.6 us
  Pallas kernels  55.2 us (94%)
  local copies, waits for them, and re-layouts  2.72 us (5%)
  between operations  0.65 us (1%)
    pallas_call x1, Pallas kernels, per_device(): pl.pallas_call(functools.partial(kernel, n_strike, n_depth), out_shape=tu...  55.2 us
    unnamed x4, local copies, waits for them, and re-layouts  2.72 us

profile of v1, /device:TPU:0, one launch (start us, length us, event | category | flops | bytes accessed | tf_op | source)
XLA Modules:
  0.0 58.6 jit_solution(2132088921293118972)
XLA Ops:
  0.6 55.2 %shard_map.104 = (f32[3,8,32,128]{3,2,1,0:T(8,128)}, f32[6,8,32,128]{3,2,1,0:T(8,128)}) custom-call(f32[3,8,32,128]{3,2,1,0:T(8,128)} %vel_in.1, f32[6,8,32,128]{3,2,1,0:T(8,128)} %str_in.1, f32[8,32,128]{2,1,0:T(8,128)} %buoy.1, f32[8,32,128]{2,1,0:T(8,128)} %lam_ref.1, f32[8,32,128]{2,1,0:T(8,128)} %mu_ref.1, f32[64,8,128]{2,1,0:T(8,128)} %past.1, ...), custom_call_target="tpu_custom_call" | custom-call | tf_op jit(solution)/shard_map/pallas_call | solution.py:366
  55.9 0.0 copy-start
  55.9 1.8 %copy.13 = f32[3,8,32,128]{3,2,1,0:T(8,128)} copy(f32[3,8,32,128]{3,2,1,0:T(8,128)} %get-tuple-element.4) | data formatting | bytes 786432
  57.7 0.0 copy-done
  57.7 0.9 %copy.14 = f32[6,8,32,128]{3,2,1,0:T(8,128)} copy(f32[6,8,32,128]{3,2,1,0:T(8,128)S(1)} %copy-done) | data formatting | bytes 1572864
Async XLA Ops:
  55.9 1.9 %copy-start = (f32[6,8,32,128]{3,2,1,0:T(8,128)S(1)}, f32[6,8,32,128]{3,2,1,0:T(8,128)}, u32[]{:S(2)}) copy-start(f32[6,8,32,128]{3,2,1,0:T(8,128)} %get-tuple-element.5) | copy-start | bytes 2359300

commit v2 on v1

--- a/solution.py
+++ b/solution.py
@@ -21,15 +21,21 @@
     n_depth,
     vel_in,
     str_in,
+    buoy_in,
+    lam_in,
+    mu_in,
+    past_in,
+    coefs,
+    prestress_in,
+    mask_in,
+    vel,
+    stress,
     buoy,
     lam_ref,
     mu_ref,
     past,
-    coefs,
     prestress,
     mask,
-    vel,
-    stress,
     pack0,
     pack1,
     accs,
@@ -47,10 +53,29 @@
     layer_coef,
     send_sem,
     recv_sem,
+    load_sem,
 ):
     nz, ny, nx = buoy.shape
     y0 = ny // 2
     hist = past.shape[0]
+    loads = [
+        pltpu.make_async_copy(src, dst, load_sem.at[i])
+        for i, (src, dst) in enumerate(
+            (
+                (str_in, stress),
+                (lam_in, lam_ref),
+                (mu_in, mu_ref),
+                (mask_in, mask),
+                (past_in, past),
+                (vel_in, vel),
+                (buoy_in, buoy),
+                (prestress_in, prestress),
+            )
+        )
+    ]
+    for load in loads:
+        load.start()
+
     s = lax.axis_index("strike")
     d = lax.axis_index("depth")
     left = lax.rem(s + n_strike - 1, n_strike)
@@ -158,23 +183,25 @@
         got_b[...] = jnp.zeros_like(got_b)
         got_rb[...] = jnp.zeros_like(got_rb)
 
-    stage[0, 0] = str_in[4, 0]
+    for load in loads[:4]:
+        load.wait()
+    stage[0, 0] = stress[4, 0]
     stage[0, 1] = lam_ref[0]
     stage[0, 2] = mu_ref[0]
-    stage[1, 0] = str_in[2, nz - 1]
-    stage[1, 1] = str_in[3, nz - 1]
+    stage[1, 0] = stress[2, nz - 1]
+    stage[1, 1] = stress[3, nz - 1]
     stage[1, 2] = mu_ref[nz - 1]
     heads, tails = [], []
     for z in range(nz):
         heads += [
-            (z, str_in[0, z][:, :1]),
+            (z, stress[0, z][:, :1]),
             (GROUP + z, lam_ref[z][:, :1]),
             (2 * GROUP + z, mu_ref[z][:, :1]),
         ]
         slides = mask[z : z + 1, :].astype(F32)
         tails += [
-            (z, str_in[1, z][:, nx - 1 :]),
-            (GROUP + z, str_in[2, z][:, nx - 1 :]),
+            (z, stress[1, z][:, nx - 1 :]),
+            (GROUP + z, stress[2, z][:, nx - 1 :]),
             (2 * GROUP + z, mu_ref[z][:, nx - 1 :]),
             (3 * GROUP + z, slides[:, nx - 1 :]),
         ]
@@ -187,8 +214,8 @@
     for kind, source in opening:
         start(kind, 1, source)
 
-    vel[...] = vel_in[...]
-    stress[...] = str_in[...]
+    for load in loads[4:]:
+        load.wait()
 
     def add_past(m, sums):
         plane = past[m]
@@ -282,17 +309,63 @@
         def _():
             copy(6, slot).start()
 
-        for kind in range(6):
-            finish(kind, slot)
+        def strain(z, low_z, top_x, top_y):
+            vx, vy, vz = vel[0, z], vel[1, z], vel[2, z]
+            vz_below = low_z if z == 0 else vel[2, z - 1]
+            vx_above = top_x if z == nz - 1 else vel[0, z + 1]
+            vy_above = top_y if z == nz - 1 else vel[1, z + 1]
+            lam, mu = DT * lam_ref[z], DT * mu_ref[z]
+            twice = 2.0 * mu
+            strain_x = vx - behind_x(vx, 0.0)
+            strain_y = vy - behind_y(vy)
+            strain_z = vz - vz_below
+            spread = lam * (strain_x + strain_y + strain_z)
+            stress[0, z] = stress[0, z] + (twice * strain_x + spread)
+            stress[5, z] = stress[5, z] + (twice * strain_y + spread)
+            stress[4, z] = stress[4, z] + (twice * strain_z + spread)
+            stress[1, z] = stress[1, z] + mu * (ahead_y(vx) - vx + (ahead_x(vy, 0.0) - vy))
+            stress[2, z] = stress[2, z] + mu * (vx_above - vx + (ahead_x(vz, 0.0) - vz))
+            stress[3, z] = stress[3, z] + mu * (vy_above - vy + (ahead_y(vz) - vz))
+
+        for z in range(1, nz - 1):
+            strain(z, None, None, None)
+        finish(4, slot)
+        finish(5, slot)
+        top_x, top_y, top_z = got_t[slot, 0], got_t[slot, 1], got_t[slot, 2]
+        low_x, low_y, low_z = got_b[slot, 0], got_b[slot, 1], got_b[slot, 2]
+        strain(0, low_z, top_x, top_y)
+        strain(nz - 1, low_z, top_x, top_y)
+
+        finish(0, slot)
+        finish(1, slot)
+        column_r, column_l = got_r[slot], got_l[slot]
+        for z in range(nz):
+            lam, mu = DT * lam_ref[z], DT * mu_ref[z]
+            behind = jnp.where(first_lane, -col(column_l, 0, z), 0.0)
+            spread = lam * behind
+            stress[0, z] = stress[0, z] + (2.0 * mu * behind + spread)
+            stress[5, z] = stress[5, z] + spread
+            stress[4, z] = stress[4, z] + spread
+            sxy = stress[1, z] + mu * jnp.where(last_lane, col(column_r, 1, z), 0.0)
+            stress[1, z] = sxy
+            stress[1, z, y0 : y0 + 1] = jnp.where(
+                mask[z : z + 1] == 1, fault[z : z + 1], sxy[y0 : y0 + 1]
+            )
+            stress[2, z] = stress[2, z] + mu * jnp.where(
+                last_lane, col(column_r, 2, z), 0.0
+            )
+
+        finish(2, slot)
+        finish(3, slot)
 
         @pl.when(j < STEPS - 1)
         def _():
             finish(6, slot)
 
         got_first = jnp.where(
-            lane == 2 * GROUP - 1, lanes_down(got_rb[slot], nz), got_r[slot]
-        )
-        got_last = jnp.where(lane == nz, pltpu.roll(got_lt[slot], nz, 1), got_l[slot])
+            lane == 2 * GROUP - 1, lanes_down(got_rb[slot], nz), column_r
+        )
+        got_last = jnp.where(lane == nz, pltpu.roll(got_lt[slot], nz, 1), column_l)
 
         lam_r, mu_r, mu_l = col_coef[0], col_coef[1], col_coef[2]
         strain_x = got_first - own_last
@@ -312,13 +385,11 @@
             lanes_down(got_last, 1) - got_last + lanes_down(jump, 2 * GROUP)
         )
 
-        top_x, top_y, top_z = got_t[slot, 0], got_t[slot, 1], got_t[slot, 2]
         lam_t, mu_t = layer_coef[0], layer_coef[1]
         layer_state[0] = layer_state[0] + DT * (
             (lam_t + 2.0 * mu_t) * (top_z - vel[2, nz - 1])
             + lam_t * (top_x - behind_x(top_x, col(got_last, 0, nz)) + (top_y - behind_y(top_y)))
         )
-        low_x, low_y, low_z = got_b[slot, 0], got_b[slot, 1], got_b[slot, 2]
         low_mu = DT * layer_coef[2]
         layer_state[1] = layer_state[1] + low_mu * (
             vel[0, 0] - low_x + (ahead_x(low_z, col(got_first, 2, -1)) - low_z)
@@ -326,32 +397,6 @@
         layer_state[2] = layer_state[2] + low_mu * (
             vel[1, 0] - low_y + (ahead_y(low_z) - low_z)
         )
-
-        for z in range(nz):
-            vx, vy, vz = vel[0, z], vel[1, z], vel[2, z]
-            vz_below = low_z if z == 0 else vel[2, z - 1]
-            vx_above = top_x if z == nz - 1 else vel[0, z + 1]
-            vy_above = top_y if z == nz - 1 else vel[1, z + 1]
-            lam, mu = DT * lam_ref[z], DT * mu_ref[z]
-            twice = 2.0 * mu
-            strain_x = vx - behind_x(vx, col(got_last, 0, z))
-            strain_y = vy - behind_y(vy)
-            strain_z = vz - vz_below
-            spread = lam * (strain_x + strain_y + strain_z)
-            stress[0, z] = stress[0, z] + (twice * strain_x + spread)
-            stress[5, z] = stress[5, z] + (twice * strain_y + spread)
-            stress[4, z] = stress[4, z] + (twice * strain_z + spread)
-            sxy = stress[1, z] + mu * (
-                ahead_y(vx) - vx + (ahead_x(vy, col(got_first, 1, z)) - vy)
-            )
-            stress[1, z] = sxy
-            stress[1, z, y0 : y0 + 1] = jnp.where(
-                mask[z : z + 1] == 1, fault[z : z + 1], sxy[y0 : y0 + 1]
-            )
-            stress[2, z] = stress[2, z] + mu * (
-                vx_above - vx + (ahead_x(vz, col(got_first, 2, z)) - vz)
-            )
-            stress[3, z] = stress[3, z] + mu * (vy_above - vy + (ahead_y(vz) - vz))
         return carry
 
     lax.fori_loop(0, STEPS, step, 0)
@@ -361,7 +406,7 @@
     nz, ny, nx = args[2].shape
     slab = (2, ny, nx)
     vmem = pl.BlockSpec(memory_space=pltpu.VMEM)
-    specs = [vmem] * len(args)
+    specs = [pl.BlockSpec(memory_space=pl.ANY)] * len(args)
     specs[6] = pl.BlockSpec(memory_space=pltpu.SMEM)
     return pl.pallas_call(
         functools.partial(kernel, n_strike, n_depth),
@@ -369,6 +414,7 @@
         in_specs=specs,
         out_specs=(vmem, vmem),
         scratch_shapes=[
+            *(pltpu.VMEM(args[i].shape, args[i].dtype) for i in (2, 3, 4, 5, 7, 8)),
             pltpu.VMEM(slab, F32),
             pltpu.VMEM(slab, F32),
             pltpu.VMEM((2, STEPS, nz, nx), F32),
@@ -386,6 +432,7 @@
             pltpu.VMEM((3, ny, nx), F32),
             pltpu.SemaphoreType.DMA((7, 2)),
             pltpu.SemaphoreType.DMA((7, 2)),
+            pltpu.SemaphoreType.DMA((8,)),
         ],
         compiler_params=pltpu.CompilerParams(collective_id=0, has_side_effects=True),
     )(*args)

time: 58.8 us -> 56.3 us (0.957)
  Pallas kernels: 55.2 us -> 52.8 us
    pallas_call x1, Pallas kernels: 55.2 us -> 52.8 us  [per_device(): pl.pallas_call(functools.partial(kernel, n_strike, n_depth), out_shape=tu...]
where the time goes in v2:
time: 56.3 us; the launch traced here: 56.2 us
  Pallas kernels  52.8 us (94%)
  local copies, waits for them, and re-layouts  2.72 us (5%)
  between operations  0.65 us (1%)
    pallas_call x1, Pallas kernels, per_device(): pl.pallas_call(functools.partial(kernel, n_strike, n_depth), out_shape=tu...  52.8 us
    unnamed x4, local copies, waits for them, and re-layouts  2.72 us

profile of v2, /device:TPU:0, one launch (start us, length us, event | category | flops | bytes accessed | tf_op | source)
XLA Modules:
  0.0 56.2 jit_solution(1176587113439212735)
XLA Ops:
  0.6 52.8 %shard_map.104 = (f32[3,8,32,128]{3,2,1,0:T(8,128)}, f32[6,8,32,128]{3,2,1,0:T(8,128)}) custom-call(f32[3,8,32,128]{3,2,1,0:T(8,128)} %vel_in.1, f32[6,8,32,128]{3,2,1,0:T(8,128)} %str_in.1, f32[8,32,128]{2,1,0:T(8,128)} %buoy_in.1, f32[8,32,128]{2,1,0:T(8,128)} %lam_in.1, f32[8,32,128]{2,1,0:T(8,128)} %mu_in.1, f32[64,8,128]{2,1,0:T(8,128)} %past_in.1, ...), custom_call_target="tpu_custom_call" | custom-call | tf_op jit(solution)/shard_map/pallas_call | solution.py:411
  53.4 0.0 copy-start
  53.5 1.8 %copy.13 = f32[3,8,32,128]{3,2,1,0:T(8,128)} copy(f32[3,8,32,128]{3,2,1,0:T(8,128)} %get-tuple-element.4) | data formatting | bytes 786432
  55.3 0.0 copy-done
  55.3 0.9 %copy.14 = f32[6,8,32,128]{3,2,1,0:T(8,128)} copy(f32[6,8,32,128]{3,2,1,0:T(8,128)S(1)} %copy-done) | data formatting | bytes 1572864
Async XLA Ops:
  53.4 1.9 %copy-start = (f32[6,8,32,128]{3,2,1,0:T(8,128)S(1)}, f32[6,8,32,128]{3,2,1,0:T(8,128)}, u32[]{:S(2)}) copy-start(f32[6,8,32,128]{3,2,1,0:T(8,128)} %get-tuple-element.5) | copy-start | bytes 2359300

commit v3 on v2

--- a/solution.py
+++ b/solution.py
@@ -254,9 +254,8 @@
     def step(j, carry):
         slot = lax.rem(j, 2)
         other = 1 - slot
-        sxx_r, sxy_l, sxz_l = col_state[0], col_state[1], col_state[2]
-
         def velocity(z):
+            sxx_r, sxy_l, sxz_l = col_state[0], col_state[1], col_state[2]
             sxx, sxy, sxz = stress[0, z], stress[1, z], stress[2, z]
             syz, szz, syy = stress[3, z], stress[4, z], stress[5, z]
             sxz_below = layer_state[1] if z == 0 else stress[2, z - 1]
@@ -273,12 +272,32 @@
                 sxz - behind_x(sxz, col(sxz_l, 0, z)) + (syz - behind_y(syz)) + (szz_above - szz)
             )
 
+        for z in range(1, nz - 1):
+            velocity(z)
+
+        @pl.when(j > 0)
+        def _():
+            for kind in (2, 3, 6):
+                finish(kind, other)
+            vz_corner, vx_corner = got_rb[other], got_lt[other]
+            at = 2 * GROUP + nz - 1
+            col_state[0] = col_state[0] - DT * col_coef[0] * jnp.where(
+                first_lane, vz_corner[:, at : at + 1], 0.0
+            )
+            col_state[2] = col_state[2] + DT * col_coef[2] * jnp.where(
+                lane == nz - 1, vx_corner[:, :1], 0.0
+            )
+            layer_state[0] = layer_state[0] - DT * layer_coef[0] * jnp.where(
+                first_lane, vx_corner[:, :1], 0.0
+            )
+            layer_state[1] = layer_state[1] + DT * layer_coef[2] * jnp.where(
+                last_lane, vz_corner[:, at : at + 1], 0.0
+            )
+
         velocity(0)
         start(4, slot)
         velocity(nz - 1)
         start(5, slot)
-        for z in range(1, nz - 1):
-            velocity(z)
 
         rate = jnp.concatenate(
             [vel[0, z, y0 + 1 : y0 + 2] - vel[0, z, y0 : y0 + 1] for z in range(nz)], axis=0
@@ -302,12 +321,11 @@
         pack1[slot] = own_last
         start(1, slot)
         start(0, slot)
-        start(2, slot)
-        start(3, slot)
 
         @pl.when(j < STEPS - 1)
         def _():
-            copy(6, slot).start()
+            for kind in (2, 3, 6):
+                start(kind, slot)
 
         def strain(z, low_z, top_x, top_y):
             vx, vy, vz = vel[0, z], vel[1, z], vel[2, z]
@@ -355,44 +373,34 @@
                 last_lane, col(column_r, 2, z), 0.0
             )
 
-        finish(2, slot)
-        finish(3, slot)
-
-        @pl.when(j < STEPS - 1)
-        def _():
-            finish(6, slot)
-
-        got_first = jnp.where(
-            lane == 2 * GROUP - 1, lanes_down(got_rb[slot], nz), column_r
-        )
-        got_last = jnp.where(lane == nz, pltpu.roll(got_lt[slot], nz, 1), column_l)
+        got_first, got_last = column_r, column_l
 
         lam_r, mu_r, mu_l = col_coef[0], col_coef[1], col_coef[2]
         strain_x = got_first - own_last
         strain_y = lanes_down(got_first - behind_y(got_first), GROUP)
         strain_z = lanes_down(got_first - pltpu.roll(got_first, 1, 1), 2 * GROUP)
-        col_state[0] = sxx_r + DT * (
+        col_state[0] = col_state[0] + DT * (
             (lam_r + 2.0 * mu_r) * strain_x + lam_r * (strain_y + strain_z)
         )
         jump = own_first - got_last
-        sheared = sxy_l + DT * mu_l * (ahead_y(got_last) - got_last + lanes_down(jump, GROUP))
+        sheared = col_state[1] + DT * mu_l * (ahead_y(got_last) - got_last + lanes_down(jump, GROUP))
         col_state[1] = jnp.where(
             jnp.logical_and(row == y0, col_coef[3] > 0.5),
             lanes_down(got_last, 3 * GROUP),
             sheared,
         )
-        col_state[2] = sxz_l + DT * mu_l * (
+        col_state[2] = col_state[2] + DT * mu_l * (
             lanes_down(got_last, 1) - got_last + lanes_down(jump, 2 * GROUP)
         )
 
         lam_t, mu_t = layer_coef[0], layer_coef[1]
         layer_state[0] = layer_state[0] + DT * (
             (lam_t + 2.0 * mu_t) * (top_z - vel[2, nz - 1])
-            + lam_t * (top_x - behind_x(top_x, col(got_last, 0, nz)) + (top_y - behind_y(top_y)))
+            + lam_t * (top_x - behind_x(top_x, 0.0) + (top_y - behind_y(top_y)))
         )
         low_mu = DT * layer_coef[2]
         layer_state[1] = layer_state[1] + low_mu * (
-            vel[0, 0] - low_x + (ahead_x(low_z, col(got_first, 2, -1)) - low_z)
+            vel[0, 0] - low_x + (ahead_x(low_z, 0.0) - low_z)
         )
         layer_state[2] = layer_state[2] + low_mu * (
             vel[1, 0] - low_y + (ahead_y(low_z) - low_z)

time: 56.3 us -> 53.9 us (0.957)
  Pallas kernels: 52.8 us -> 50.4 us
    pallas_call x1, Pallas kernels: 52.8 us -> 50.4 us  [per_device(): pl.pallas_call(functools.partial(kernel, n_strike, n_depth), out_shape=tu...]
where the time goes in v3:
time: 53.9 us; the launch traced here: 53.8 us
  Pallas kernels  50.4 us (94%)
  local copies, waits for them, and re-layouts  2.72 us (5%)
  between operations  0.65 us (1%)
    pallas_call x1, Pallas kernels, per_device(): pl.pallas_call(functools.partial(kernel, n_strike, n_depth), out_shape=tu...  50.4 us
    unnamed x4, local copies, waits for them, and re-layouts  2.72 us

profile of v3, /device:TPU:0, one launch (start us, length us, event | category | flops | bytes accessed | tf_op | source)
XLA Modules:
  0.0 53.8 jit_solution(15108416409764382526)
XLA Ops:
  0.6 50.4 %shard_map.104 = (f32[3,8,32,128]{3,2,1,0:T(8,128)}, f32[6,8,32,128]{3,2,1,0:T(8,128)}) custom-call(f32[3,8,32,128]{3,2,1,0:T(8,128)} %vel_in.1, f32[6,8,32,128]{3,2,1,0:T(8,128)} %str_in.1, f32[8,32,128]{2,1,0:T(8,128)} %buoy_in.1, f32[8,32,128]{2,1,0:T(8,128)} %lam_in.1, f32[8,32,128]{2,1,0:T(8,128)} %mu_in.1, f32[64,8,128]{2,1,0:T(8,128)} %past_in.1, ...), custom_call_target="tpu_custom_call" | custom-call | tf_op jit(solution)/shard_map/pallas_call | solution.py:419
  51.0 0.0 copy-start
  51.1 1.8 %copy.13 = f32[3,8,32,128]{3,2,1,0:T(8,128)} copy(f32[3,8,32,128]{3,2,1,0:T(8,128)} %get-tuple-element.4) | data formatting | bytes 786432
  52.9 0.0 copy-done
  52.9 0.9 %copy.14 = f32[6,8,32,128]{3,2,1,0:T(8,128)} copy(f32[6,8,32,128]{3,2,1,0:T(8,128)S(1)} %copy-done) | data formatting | bytes 1572864
Async XLA Ops:
  51.0 1.9 %copy-start = (f32[6,8,32,128]{3,2,1,0:T(8,128)S(1)}, f32[6,8,32,128]{3,2,1,0:T(8,128)}, u32[]{:S(2)}) copy-start(f32[6,8,32,128]{3,2,1,0:T(8,128)} %get-tuple-element.5) | copy-start | bytes 2359300

commit v4 on v3

--- a/solution.py
+++ b/solution.py
@@ -295,9 +295,7 @@
             )
 
         velocity(0)
-        start(4, slot)
         velocity(nz - 1)
-        start(5, slot)
 
         rate = jnp.concatenate(
             [vel[0, z, y0 + 1 : y0 + 2] - vel[0, z, y0 : y0 + 1] for z in range(nz)], axis=0
@@ -321,6 +319,8 @@
         pack1[slot] = own_last
         start(1, slot)
         start(0, slot)
+        start(4, slot)
+        start(5, slot)
 
         @pl.when(j < STEPS - 1)
         def _():

time: 53.9 us -> 53.4 us (level)
  Pallas kernels: 50.4 us -> 49.8 us
    pallas_call x1, Pallas kernels: 50.4 us -> 49.8 us  [per_device(): pl.pallas_call(functools.partial(kernel, n_strike, n_depth), out_shape=tu...]
where the time goes in v4:
time: 53.4 us; the launch traced here: 53.2 us
  Pallas kernels  49.8 us (93%)
  local copies, waits for them, and re-layouts  2.72 us (5%)
  between operations  0.65 us (1%)
    pallas_call x1, Pallas kernels, per_device(): pl.pallas_call(functools.partial(kernel, n_strike, n_depth), out_shape=tu...  49.8 us
    unnamed x4, local copies, waits for them, and re-layouts  2.72 us

profile of v4, /device:TPU:0, one launch (start us, length us, event | category | flops | bytes accessed | tf_op | source)
XLA Modules:
  0.0 53.2 jit_solution(5455709798853371525)
XLA Ops:
  0.6 49.8 %shard_map.104 = (f32[3,8,32,128]{3,2,1,0:T(8,128)}, f32[6,8,32,128]{3,2,1,0:T(8,128)}) custom-call(f32[3,8,32,128]{3,2,1,0:T(8,128)} %vel_in.1, f32[6,8,32,128]{3,2,1,0:T(8,128)} %str_in.1, f32[8,32,128]{2,1,0:T(8,128)} %buoy_in.1, f32[8,32,128]{2,1,0:T(8,128)} %lam_in.1, f32[8,32,128]{2,1,0:T(8,128)} %mu_in.1, f32[64,8,128]{2,1,0:T(8,128)} %past_in.1, ...), custom_call_target="tpu_custom_call" | custom-call | tf_op jit(solution)/shard_map/pallas_call | solution.py:419
  50.5 0.0 copy-start
  50.5 1.8 %copy.13 = f32[3,8,32,128]{3,2,1,0:T(8,128)} copy(f32[3,8,32,128]{3,2,1,0:T(8,128)} %get-tuple-element.4) | data formatting | bytes 786432
  52.3 0.0 copy-done
  52.3 0.9 %copy.14 = f32[6,8,32,128]{3,2,1,0:T(8,128)} copy(f32[6,8,32,128]{3,2,1,0:T(8,128)S(1)} %copy-done) | data formatting | bytes 1572864
Async XLA Ops:
  50.5 1.9 %copy-start = (f32[6,8,32,128]{3,2,1,0:T(8,128)S(1)}, f32[6,8,32,128]{3,2,1,0:T(8,128)}, u32[]{:S(2)}) copy-start(f32[6,8,32,128]{3,2,1,0:T(8,128)} %get-tuple-element.5) | copy-start | bytes 2359300
